TPU v7x, 256 devices: a whole 4x4x8 slice. The times are simulated.
256 devices in a mesh: rows: 64 (over x, z_hi, y), feat: 4 (over z_lo, core).
Axes of the slice: x: 4, y: 4, z: 8 (z_hi: 4, z_lo: 2; z = z_hi * 2 + z_lo), core: 2. Of those that a mesh axis runs over, the one named last changes fastest.
Arguments:
- table_cells: bfloat16 [32768, 128, 128], P('rows', 'feat'), may hold values from -6 to 6
- fold_id: int32 [32768], P('rows'), may hold values from 0 to 3, as said below
- train_mask: int32 [32768], P('rows'), may hold values from 0 to 1, as said below
- inducing: bfloat16 [128, 128], replicated, may hold values from -6 to 6
- induce_proj: bfloat16 [128, 256], replicated, may hold values from -0.5 to 0.5
- induce_back: bfloat16 [128, 384], replicated, may hold values from -0.5 to 0.5
- summary_query: bfloat16 [4, 128], replicated, may hold values from -6 to 6
- row_proj: bfloat16 [128, 256], replicated, may hold values from -0.5 to 0.5
- context_proj: bfloat16 [3, 512, 512], P(None, None, 'feat'), may hold values from -0.25 to 0.25
Outputs:
- context: bfloat16 [32768, 512], P('rows', 'feat')
Inputs may be any that keep to these rules, and one draw needn't show every extreme that they name: `train_mask`: among the rows of one device (aligned blocks of 512 rows) exactly half are training rows. `fold_id`: among the training rows of each aligned block of 512 rows every fold number occurs.
All inputs are finite; a program needn't handle non-finite values.
Results may differ from a plain program's by a relative error of at most 0.03.
Values may be sent and summed in bfloat16 or wider, within the bound.
No kernel may reach another device: no remote copies, remote signals or barrier semaphores. Data moves between devices by JAX's collectives and lax.ppermute only.
A program may use at most 128 MiB of HBM per device.

v0:
```python
import math

import jax
import jax.numpy as jnp
from jax import lax
from jax.sharding import PartitionSpec as P

HEAD_DIM = 128


epsilon = 1e-06
score_scale = 0.25


def rms_normalize(value):
    value = value.astype(jnp.float32)
    return value * lax.rsqrt(jnp.mean(value * value, axis=-1, keepdims=True) + epsilon)


def local(
    table_cells,
    fold_id,
    train_mask,
    inducing,
    induce_proj,
    induce_back,
    summary_query,
    row_proj,
    context_proj,
):
    rows_here, feats_here, embed = table_cells.shape
    col_kv = jnp.einsum(
        "rfe,ek->rfk", table_cells, induce_proj, preferred_element_type=jnp.float32
    ).astype(jnp.bfloat16)
    col_keys = rms_normalize(col_kv[..., :embed]).astype(jnp.bfloat16)
    col_values = col_kv[..., embed:]
    induce_norm = rms_normalize(inducing).astype(jnp.bfloat16)
    scores = (
        jnp.einsum("me,rfe->fmr", induce_norm, col_keys, preferred_element_type=jnp.float32)
        * score_scale
    )
    weights = (jnp.exp(scores) * train_mask.astype(jnp.float32)).astype(jnp.bfloat16)
    numerator = jnp.einsum("fmr,rfe->fme", weights, col_values, preferred_element_type=jnp.float32)
    summed = lax.psum(numerator, "rows")
    induced = rms_normalize(summed).astype(jnp.bfloat16)
    point_kv = jnp.einsum(
        "fme,ek->fmk", induced, induce_back[:, embed:], preferred_element_type=jnp.float32
    ).astype(jnp.bfloat16)
    cell_query = jnp.einsum(
        "rfe,ek->rfk", table_cells, induce_back[:, :embed], preferred_element_type=jnp.float32
    ).astype(jnp.bfloat16)
    query_norm = rms_normalize(cell_query).astype(jnp.bfloat16)
    point_keys = rms_normalize(point_kv[..., :embed]).astype(jnp.bfloat16)
    cell_scores = (
        jnp.einsum("rfe,fme->rfm", query_norm, point_keys, preferred_element_type=jnp.float32)
        * score_scale
    )
    expos = jnp.exp(cell_scores)
    probs = (expos / jnp.sum(expos, axis=-1, keepdims=True)).astype(jnp.bfloat16)
    attended = jnp.einsum(
        "rfm,fme->rfe", probs, point_kv[..., embed:], preferred_element_type=jnp.float32
    )
    updated = (table_cells.astype(jnp.float32) + attended).astype(jnp.bfloat16)
    row_kv = jnp.einsum(
        "rfe,ek->rfk", updated, row_proj, preferred_element_type=jnp.float32
    ).astype(jnp.bfloat16)
    row_keys = rms_normalize(row_kv[..., :embed]).astype(jnp.bfloat16)
    summary_norm = rms_normalize(summary_query).astype(jnp.bfloat16)
    summary_scores = (
        jnp.einsum("ce,rfe->rcf", summary_norm, row_keys, preferred_element_type=jnp.float32)
        * score_scale
    )
    summary_weights = jnp.exp(summary_scores).astype(jnp.bfloat16)
    partial_value = jnp.einsum(
        "rcf,rfe->rce", summary_weights, row_kv[..., embed:], preferred_element_type=jnp.float32
    )
    totals = lax.psum(partial_value.astype(jnp.bfloat16), "feat").astype(jnp.float32)
    represent = rms_normalize(totals).astype(jnp.bfloat16).reshape(rows_here, -1)
    head_cols = context_proj.shape[2]
    heads_here = head_cols // HEAD_DIM
    projected = jnp.einsum(
        "rd,kdc->krc", represent, context_proj, preferred_element_type=jnp.float32
    ).astype(jnp.bfloat16)
    query_heads = rms_normalize(projected[0].reshape(rows_here, heads_here, HEAD_DIM)).astype(
        jnp.bfloat16
    )
    key_flat = (
        rms_normalize(projected[1].reshape(rows_here, heads_here, HEAD_DIM))
        .astype(jnp.bfloat16)
        .reshape(rows_here, head_cols)
    )
    stacked = jnp.stack([key_flat, projected[2]], axis=1)
    my_folds = fold_id.astype(jnp.float32)
    sent_codes = jnp.where(train_mask == 1, fold_id, -1).astype(jnp.bfloat16)
    empty = jnp.zeros((rows_here, heads_here, HEAD_DIM), jnp.float32)
    rows_piece = lax.all_gather(stacked, "rows", axis=0, tiled=True)
    codes_piece = lax.all_gather(sent_codes, "rows", axis=0, tiled=True)
    count = rows_piece.shape[0]
    block = math.gcd(count, 2048)

    def step(index, total):
        offset = index * block
        kv_block = lax.dynamic_slice_in_dim(rows_piece, offset, block, 0)
        code_block = lax.dynamic_slice_in_dim(codes_piece, offset, block, 0).astype(jnp.float32)
        keys_block = kv_block[:, 0].reshape(block, heads_here, HEAD_DIM)
        values_block = kv_block[:, 1].reshape(block, heads_here, HEAD_DIM)
        block_scores = (
            jnp.einsum("qhd,khd->hqk", query_heads, keys_block, preferred_element_type=jnp.float32)
            * score_scale
        )
        allow = ((code_block[None, :] >= 0.0) & (code_block[None, :] != my_folds[:, None])).astype(
            jnp.float32
        )
        block_weights = (jnp.exp(block_scores) * allow[None]).astype(jnp.bfloat16)
        return total + jnp.einsum(
            "hqk,khd->qhd", block_weights, values_block, preferred_element_type=jnp.float32
        )

    gathered = lax.fori_loop(0, count // block, step, empty)
    return rms_normalize(gathered).astype(jnp.bfloat16).reshape(rows_here, head_cols)


def solution(mesh):
    in_specs = (
        P("rows", "feat", None),
        P("rows"),
        P("rows"),
        P(),
        P(),
        P(),
        P(),
        P(),
        P(None, None, "feat"),
    )
    out_specs = P("rows", "feat")
    return jax.shard_map(local, mesh=mesh, in_specs=in_specs, out_specs=out_specs, check_vma=False)
```

profile of v0, /device:TPU:32, one launch (start us, length us, event | category | flops | bytes accessed | tf_op | source)
XLA Modules:
  0.0 1129.1 jit_solution(1551483236626328079)
XLA Ops:
  6.5 0.0 all-reduce.3.cloned.1.call-start
  6.5 7.6 copy.77
  14.1 4.6 convolution_convert_fusion.1
  18.7 0.0 copy-start.2
  18.7 3.2 copy-done.2
  21.9 0.9 fusion.10
  22.9 0.1 fusion.73
  23.0 0.0 copy-start.11
  23.0 0.0 copy-start.6
  23.1 8.4 fusion.19
  31.5 0.0 all-reduce.3.cloned.1.call-update
  31.5 0.2 all-reduce.5.cloned.1.call-start
  31.8 0.1 fusion.86
  31.9 5.5 fusion.12
  37.4 735.1 %all-reduce.3.cloned.1.call-done = f32[32,128,128]{2,1,0:T(8,128)} async-done(((f32[32,128,128]{2,1,0:T(8,128)}), f32[32,128,128]{2,1,0:T(8,128)}) %all-reduce.3.cloned.1.call-update) | async-done | bytes 2097168 | tf_op jit(solution)/shard_map/psum | solution.py:44
  772.5 2.4 multiply_reduce_fusion
  774.9 2.4 convolution_convert_fusion.3
  777.3 0.6 fusion.46
  777.9 0.0 copy-start.10
  777.9 4.4 bitcast_reduce_fusion
  782.3 9.6 convolution_convert_fusion
  792.0 4.9 slice.65
  796.9 1.2 copy-done.4
  798.1 0.9 fusion.14
  799.0 8.0 copy.92
  807.1 3.1 fusion.54
  810.2 0.0 copy-start.5
  810.2 0.3 copy.91
  810.5 4.2 convolution_convert_fusion.4
  814.7 0.0 all-reduce.5.cloned.1.call-update
  814.7 0.3 all-gather.3.cloned.1.call-start
  815.0 0.2 copy.95
  815.2 40.4 %all-reduce.5.cloned.1.call-done = bf16[512,4,128]{2,1,0:T(4,128)(2,1)} async-done(((bf16[512,4,128]{2,1,0:T(4,128)(2,1)}), bf16[512,4,128]{2,1,0:T(4,128)(2,1)}) %all-reduce.5.cloned.1.call-update) | async-done | bytes 524304 | tf_op jit(solution)/shard_map/psum | solution.py:77
  855.6 1.7 fusion.57
  857.3 1.7 fusion.58
  858.9 0.4 fusion.65
  859.3 0.1 convert_bitcast_fusion
  859.4 0.1 fusion.70
  859.6 0.7 pad_maximum_fusion
  860.3 0.0 all-gather.3.cloned.1.call-update
  860.3 213.6 %all-gather = bf16[64,1,512]{2,1,0:T(2,128)(2,1)S(1)} all-gather(bf16[1,1,512]{2,1,0:T(2,128)(2,1)S(1)} %reshape.242), channel_id=1, replica_groups=mesh['rows'=64,'feat'=4] {'rows'}, dimensions={0}, use_global_device_ids=true | all-gather | bytes 66560 | tf_op jit(solution)/shard_map/all_gather | solution.py:97
  1073.9 0.4 reduce.3
  1074.3 0.1 copy.97
  1074.4 0.0 all-gather.3.cloned.1.call-done
  1074.4 47.2 %while.14 = (s32[]{:T(128)}, f32[512,1,128]{0,2,1:T(8,128)S(1)}, bf16[32768,2,128]{0,2,1:T(8,128)(2,1)}, bf16[32768]{0:T(1024)(128)(2,1)S(1)}, f32[512]{0:T(512)...) while((s32[]{:T(128)}, f32[512,1,128]{0,2,1:T(8,128)S(1)}, ...), condition=%wide.region_14.15_spmd.clone, body=%wide.region_13.14_spmd.clone.sunk | while | flops 542251008 | bytes 1736888 | solution.py:119
  1074.5 2.9 fusion.103
  1077.4 2.9 fusion.103
  1080.4 2.9 fusion.103
  1083.3 2.9 fusion.103
  1086.3 2.9 fusion.103
  1089.2 2.9 fusion.103
  1092.2 2.9 fusion.103
  1095.1 2.9 fusion.103
  1098.1 2.9 fusion.103
  1101.0 2.9 fusion.103
  1104.0 2.9 fusion.103
  1106.9 2.9 fusion.103
  1109.9 2.9 fusion.103
  1112.8 2.9 fusion.103
  1115.8 2.9 fusion.103
  1118.7 2.9 fusion.103
  1121.6 0.0 copy-start.1
  1121.6 0.1 copy.98
  1121.8 0.8 fusion.72
  (65 shorter events, 0.7 us)
Async XLA Ops:
  6.5 7.6 copy-start
  6.5 766.0 %all-reduce.3.cloned.1.call-start = ((), (), s32[]{:S(2)}) async-start(), calls=%async_computation | async-start | bytes 4194304 | tf_op jit(solution)/shard_map/psum | solution.py:44
  18.7 3.2 copy-start.2
  21.9 1.0 copy-start.7
  21.9 1.1 copy-start.8
  21.9 1.1 copy-start.9
  23.0 8.7 copy-start.11
  23.0 8.9 copy-start.6
  31.5 824.0 %all-reduce.5.cloned.1.call-start = ((), (), s32[]{:S(2)}) async-start(), calls=%async_computation.1 | async-start | bytes 1048576 | tf_op jit(solution)/shard_map/psum | solution.py:77
  772.5 5.4 copy-start.3
  777.9 4.4 copy-start.10
  791.9 6.2 copy-start.4
  810.2 4.8 copy-start.5
  814.7 259.7 %all-gather.3.cloned.1.call-start = ((), (), s32[]{:S(2)}) async-start(), calls=%async_computation.2 | async-start | bytes 17039360 | tf_op jit(solution)/shard_map/all_gather | solution.py:96
  1121.6 1.0 copy-start.1
Sparse Core Ops, SparseCore 0:
  31.6 740.8 all-reduce.2
  814.8 40.6 all-reduce.4
  860.4 187.5 all-gather.2
where the time goes:
time: 1130 us
  waiting for transfers between devices  776 us (69%)
  blocking collectives  214 us (19%)
  matrix products  88.5 us (8%)
  local copies, waits for them, and re-layouts  25.8 us (2%)
  between operations  13.4 us (1%)
    psum x1, waiting for transfers between devices, local(): summed = lax.psum(numerator, 'rows')  735 us
    all_gather x1, blocking collectives, local(): codes_piece = lax.all_gather(sent_codes, 'rows', axis=0, tiled=True)  214 us
    dot_general x16, matrix products, step(): jnp.einsum('hqk,khd->qhd', block_weights, values_block, preferred_element...  46 us
    psum x1, waiting for transfers between devices, local(): lax.psum(partial_value.astype(jnp.bfloat16), 'feat').astype(jnp.float32)  40.4 us
  transfers between devices with their start and end apart: 3, of which 2 were waited for; matrix products, arithmetic and copies ran while one was open for 1% of the time, Pallas kernels for 0%

commit v1 on v0

v1 whole, which is shorter than its diff:
```python
import jax
import jax.numpy as jnp
from jax import lax
from jax.experimental import pallas as pl
from jax.experimental.pallas import tpu as pltpu
from jax.sharding import Mesh, PartitionSpec as P

HEAD_DIM = 128
XY = ("x", "y")
FEAT = ("zl", "core")
KEY_GROUP = ("x", "y", "zl", "core")
QUERY_GROUP = ("zh", "zl", "core")

epsilon = 1e-06
score_scale = 0.25
LOG2E = 1.4426950408889634
FOLD_PENALTY = 16384.0


def rms_normalize(value):
    value = value.astype(jnp.float32)
    return value * lax.rsqrt(jnp.mean(value * value, axis=-1, keepdims=True) + epsilon)


def exchange(value, axes):
    return lax.all_to_all(value, axes, 0, 0, tiled=True)


def attention_kernel(q_ref, k_ref, v_ref, o_ref, *, key_block):
    q = q_ref[...]
    total = jnp.zeros(o_ref.shape, jnp.float32)
    for start in range(0, k_ref.shape[0], key_block):
        scores = lax.dot_general(
            q,
            k_ref[start : start + key_block, :],
            (((1,), (1,)), ((), ())),
            preferred_element_type=jnp.float32,
        )
        weights = jnp.exp2(scores).astype(jnp.bfloat16)
        total = total + jnp.dot(
            weights, v_ref[start : start + key_block, :], preferred_element_type=jnp.float32
        )
    o_ref[...] = total.astype(o_ref.dtype)


def attention(q, k, v, query_block=512, key_block=512):
    queries, width = q.shape
    keys = k.shape[0]
    return pl.pallas_call(
        lambda *refs: attention_kernel(*refs, key_block=key_block),
        out_shape=jax.ShapeDtypeStruct((queries, HEAD_DIM), jnp.bfloat16),
        grid=(queries // query_block,),
        in_specs=[
            pl.BlockSpec((query_block, width), lambda i: (i, 0)),
            pl.BlockSpec((keys, width), lambda i: (0, 0)),
            pl.BlockSpec((keys, HEAD_DIM), lambda i: (0, 0)),
        ],
        out_specs=pl.BlockSpec((query_block, HEAD_DIM), lambda i: (i, 0)),
        name="attention",
    )(q, k, v)


def other(value, axis):
    return lax.ppermute(value, axis, [(0, 1), (1, 0)])


def local(
    table_cells,
    fold_id,
    train_mask,
    inducing,
    induce_proj,
    induce_back,
    summary_query,
    row_proj,
    context_proj,
):
    rows_here, feats_here, embed = table_cells.shape
    width = context_proj.shape[1]
    zl = lax.axis_index("zl")
    core = lax.axis_index("core")
    zh = lax.axis_index("zh")
    xy = lax.axis_index("x") * lax.axis_size("y") + lax.axis_index("y")
    groups_xy = lax.axis_size("x") * lax.axis_size("y")
    groups_z = lax.axis_size("zh")
    feat_devices = lax.axis_size("zl") * lax.axis_size("core")
    block = rows_here // feat_devices
    half = block // 2

    proj_pair = jnp.concatenate([context_proj, other(context_proj, "core")], axis=2)
    proj_full = jnp.concatenate([proj_pair, other(proj_pair, "zl")], axis=2)

    labelled = (train_mask == 1).astype(jnp.bfloat16)
    index = jnp.arange(rows_here)
    before = (index[:, None] < index[None, :]).astype(jnp.bfloat16)
    rank_train = jnp.dot(labelled[None], before, preferred_element_type=jnp.float32)[0].astype(
        jnp.int32
    )
    rank = jnp.where(train_mask == 1, rank_train, index - rank_train)
    slot = (rank // half) * block + rank % half + jnp.where(train_mask == 1, 0, half)
    permute = (index[:, None] == slot[None, :]).astype(jnp.bfloat16)
    codes = jnp.dot(
        permute, fold_id.astype(jnp.bfloat16)[:, None], preferred_element_type=jnp.float32
    ).astype(jnp.bfloat16)
    codes = codes.reshape(feat_devices, block)

    col_kv = jnp.einsum(
        "rfe,ek->rfk", table_cells, induce_proj, preferred_element_type=jnp.float32
    ).astype(jnp.bfloat16)
    col_keys = rms_normalize(col_kv[..., :embed]).astype(jnp.bfloat16)
    col_values = col_kv[..., embed:]
    induce_norm = rms_normalize(inducing).astype(jnp.bfloat16)
    scores = (
        jnp.einsum("me,rfe->fmr", induce_norm, col_keys, preferred_element_type=jnp.float32)
        * score_scale
    )
    weights = (jnp.exp(scores) * train_mask.astype(jnp.float32)).astype(jnp.bfloat16)
    numerator = jnp.einsum(
        "fmr,rfe->fme", weights, col_values, preferred_element_type=jnp.float32
    ).astype(jnp.bfloat16)

    points = inducing.shape[0]
    share_xy = feats_here * points // groups_xy
    share = share_xy // groups_z
    part = exchange(numerator.reshape(groups_xy, share_xy, embed), XY)
    part = jnp.sum(part.astype(jnp.float32), axis=0).astype(jnp.bfloat16)
    part = exchange(part.reshape(groups_z, share, embed), "zh")
    mine = rms_normalize(jnp.sum(part.astype(jnp.float32), axis=0)).astype(jnp.bfloat16)
    sent = jnp.concatenate([mine, jnp.pad(codes, ((0, 12), (0, 0)))], axis=0)
    got = exchange(jnp.broadcast_to(sent[None], (groups_z,) + sent.shape), "zh")
    sent = jnp.concatenate(
        [got[:, :share].reshape(share_xy, embed), got[:, share : share + 4].reshape(-1, embed)],
        axis=0,
    )
    got = exchange(jnp.broadcast_to(sent[None], (groups_xy,) + sent.shape), XY)
    induced = got[:, :share_xy].reshape(feats_here, points, embed)
    all_codes = got[:, share_xy:].reshape(groups_xy, groups_z, feat_devices, block)

    point_kv = jnp.einsum(
        "fme,ek->fmk", induced, induce_back[:, embed:], preferred_element_type=jnp.float32
    ).astype(jnp.bfloat16)
    cell_query = jnp.einsum(
        "rfe,ek->rfk", table_cells, induce_back[:, :embed], preferred_element_type=jnp.float32
    ).astype(jnp.bfloat16)
    query_norm = rms_normalize(cell_query).astype(jnp.bfloat16)
    point_keys = rms_normalize(point_kv[..., :embed]).astype(jnp.bfloat16)
    cell_scores = (
        jnp.einsum("rfe,fme->rfm", query_norm, point_keys, preferred_element_type=jnp.float32)
        * score_scale
    )
    expos = jnp.exp(cell_scores)
    probs = (expos / jnp.sum(expos, axis=-1, keepdims=True)).astype(jnp.bfloat16)
    attended = jnp.einsum(
        "rfm,fme->rfe", probs, point_kv[..., embed:], preferred_element_type=jnp.float32
    )
    updated = (table_cells.astype(jnp.float32) + attended).astype(jnp.bfloat16)
    row_kv = jnp.einsum(
        "rfe,ek->rfk", updated, row_proj, preferred_element_type=jnp.float32
    ).astype(jnp.bfloat16)
    row_keys = rms_normalize(row_kv[..., :embed]).astype(jnp.bfloat16)
    summary_norm = rms_normalize(summary_query).astype(jnp.bfloat16)
    summary_scores = (
        jnp.einsum("ce,rfe->rcf", summary_norm, row_keys, preferred_element_type=jnp.float32)
        * score_scale
    )
    summary_weights = jnp.exp(summary_scores).astype(jnp.bfloat16)
    partial_value = jnp.einsum(
        "rcf,rfe->rce", summary_weights, row_kv[..., embed:], preferred_element_type=jnp.float32
    ).astype(jnp.bfloat16)

    ordered = jnp.dot(
        permute, partial_value.reshape(rows_here, width), preferred_element_type=jnp.float32
    ).astype(jnp.bfloat16)
    got = exchange(ordered.reshape(feat_devices, block, width), FEAT)
    totals = jnp.sum(got.astype(jnp.float32), axis=0)
    represent = rms_normalize(totals.reshape(block, -1, embed)).astype(jnp.bfloat16)
    projected = jnp.einsum(
        "rd,kdc->krc",
        represent.reshape(block, width),
        proj_full,
        preferred_element_type=jnp.float32,
    ).astype(jnp.bfloat16)

    def heads(value):
        value = value.reshape(-1, 2, 2, HEAD_DIM).transpose(1, 2, 0, 3)
        value = jnp.where(zl == 0, value, value[::-1])
        return jnp.where(core == 0, value, value[:, ::-1]).reshape(
            feat_devices, -1, HEAD_DIM
        )

    q = (rms_normalize(heads(projected[0])) * (score_scale * LOG2E)).astype(jnp.bfloat16)
    k = rms_normalize(heads(projected[1][:half])).astype(jnp.bfloat16)
    v = heads(projected[2][:half])
    q_all = exchange(
        jnp.broadcast_to(q[None], (groups_z,) + q.shape).reshape(-1, block, HEAD_DIM), QUERY_GROUP
    ).reshape(-1, HEAD_DIM)
    kv = jnp.concatenate([k, v], axis=1)
    kv_all = exchange(
        jnp.broadcast_to(kv[None], (groups_xy,) + kv.shape).reshape(-1, 2 * half, HEAD_DIM),
        KEY_GROUP,
    )
    k_all = kv_all[:, :half].reshape(-1, HEAD_DIM)
    v_all = kv_all[:, half:].reshape(-1, HEAD_DIM)
    query_codes = lax.dynamic_index_in_dim(all_codes, xy, 0, keepdims=False).reshape(-1)
    key_codes = lax.dynamic_index_in_dim(all_codes, zh, 1, keepdims=False)[..., :half].reshape(-1)
    lanes = jnp.arange(HEAD_DIM).astype(jnp.float32)
    query_marks = jnp.where(
        query_codes.astype(jnp.float32)[:, None] == lanes[None], -FOLD_PENALTY, 0.0
    ).astype(jnp.bfloat16)
    key_marks = (key_codes.astype(jnp.float32)[:, None] == lanes[None]).astype(jnp.bfloat16)
    summed = attention(
        jnp.concatenate([q_all, query_marks], axis=1),
        jnp.concatenate([k_all, key_marks], axis=1),
        v_all,
    )
    got = exchange(summed.reshape(groups_z, rows_here, HEAD_DIM), "zh")
    context = rms_normalize(jnp.sum(got.astype(jnp.float32), axis=0)).astype(jnp.bfloat16)
    return lax.dot_general(
        permute, context, (((0,), (0,)), ((), ())), preferred_element_type=jnp.float32
    ).astype(jnp.bfloat16)


def solution(mesh):
    fine = Mesh(mesh.devices.reshape(4, 4, 4, 2, 2), ("x", "zh", "y", "zl", "core"))
    rows = ("x", "zh", "y")
    in_specs = (
        P(rows, FEAT, None),
        P(rows),
        P(rows),
        P(),
        P(),
        P(),
        P(),
        P(),
        P(None, None, FEAT),
    )
    return jax.shard_map(
        local, mesh=fine, in_specs=in_specs, out_specs=P(rows, FEAT), check_vma=False
    )
```

time: 1130 us -> 265 us (0.23)
  waiting for transfers between devices: 776 us -> 93 us
  blocking collectives: 214 us -> 28.2 us
  matrix products: 88.5 us -> 43.9 us
  starting transfers between devices: 0.49 us -> 35.6 us
  Pallas kernels: 0 us -> 13.7 us
  between operations: 13.4 us -> 0.51 us
    psum x2 -> x0, waiting for transfers between devices: 776 us -> none  [the longest x1 735 us: local(): summed = lax.psum(numerator, 'rows')]
    all_gather x1 -> x0, blocking collectives: 214 us -> none  [local(): codes_piece = lax.all_gather(sent_codes, 'rows', axis=0, tiled=True)]
    all_to_all x0 -> x6, waiting for transfers between devices: none -> 76.7 us  [exchange(): return lax.all_to_all(value, axes, 0, 0, tiled=True)]
    dot_general x16 -> x5, matrix products: 46 us -> 4.66 us  [the longest x1 1.73 us: local(): jnp.einsum('rd,kdc->krc', represent.reshape(block, width), proj_full, pre...]
    all_to_all x0 -> x6, starting transfers between devices: none -> 35 us  [exchange(): return lax.all_to_all(value, axes, 0, 0, tiled=True)]
    all_to_all x0 -> x2, blocking collectives: none -> 28.2 us  [exchange(): return lax.all_to_all(value, axes, 0, 0, tiled=True)]
    ppermute x0 -> x2, waiting for transfers between devices: none -> 16.3 us  [other(): return lax.ppermute(value, axis, [(0, 1), (1, 0)])]
    pallas_call x0 -> x1, Pallas kernels: none -> 13.7 us  [attention(): pl.pallas_call(lambda *refs: attention_kernel(*refs, key_block=key_block)...]
  transfers between devices with their start and end apart: 3 -> 8, of which waited for: 2 -> 7; matrix products, arithmetic and copies ran while one was open for 1% -> 19% of each run, Pallas kernels for 0% -> 0%
where the time goes in v1:
time: 265 us; the launch traced here: 260 us
  waiting for transfers between devices  93 us (35%)
  matrix products  43.9 us (17%)
  starting transfers between devices  35.6 us (13%)
  local copies, waits for them, and re-layouts  33.5 us (13%)
  blocking collectives  28.2 us (11%)
  Pallas kernels  13.7 us (5%)
  other arithmetic  11.8 us (4%)
    all_to_all x6, waiting for transfers between devices, exchange(): return lax.all_to_all(value, axes, 0, 0, tiled=True)  76.7 us
    all_to_all x6, starting transfers between devices, exchange(): return lax.all_to_all(value, axes, 0, 0, tiled=True)  35 us
    all_to_all x2, blocking collectives, exchange(): return lax.all_to_all(value, axes, 0, 0, tiled=True)  28.2 us
    ppermute x2, waiting for transfers between devices, other(): return lax.ppermute(value, axis, [(0, 1), (1, 0)])  16.3 us
    pallas_call x1, Pallas kernels, attention(): pl.pallas_call(lambda *refs: attention_kernel(*refs, key_block=key_block)...  13.7 us
    slice x2, local copies, waits for them, and re-layouts, local(): row_kv[..., embed:]  12.9 us
    unnamed x25, local copies, waits for them, and re-layouts  12.8 us
    dot_general x1, matrix products, local(): jnp.einsum('rfe,ek->rfk', updated, row_proj, preferred_element_type=jnp.f...  9.61 us
  transfers between devices with their start and end apart: 8, of which 7 were waited for; matrix products, arithmetic and copies ran while one was open for 19% of the time, Pallas kernels for 0%

profile of v1, /device:TPU:32, one launch (start us, length us, event | category | flops | bytes accessed | tf_op | source)
XLA Modules:
  0.0 260.1 jit_solution(11575744110063623923)
XLA Ops:
  0.0 7.6 %copy.101 = bf16[512,32,128]{0,2,1:T(8,128)(2,1)} copy(bf16[512,32,128]{2,1,0:T(8,128)(2,1)} %param.9) | data formatting | bytes 8388608 | tf_op args[0]
  7.6 4.6 %convolution_convert_fusion.1 = bf16[512,32,256]{0,2,1:T(8,128)(2,1)S(1)} fusion(bf16[512,32,128]{0,2,1:T(8,128)(2,1)} %copy.101, bf16[128,256]{1,0:T(8,128)(2,1)S(1)} %copy-done), kind=kOutput, calls=%fused_computation.20 | convolution fusion | flops 1077936128 | bytes 12648448 | tf_op jit(solution)/shard_map/rfe,ek->rfk/dot_general | solution.py:107
  12.2 3.2 %copy-done.2 = bf16[512,32,256]{0,2,1:T(8,128)(2,1)} copy-done((bf16[512,32,256]{0,2,1:T(8,128)(2,1)}, bf16[512,32,256]{0,2,1:T(8,128)(2,1)S(1)}, u32[]{:S(2)}) %copy-start.2) | copy-done | bytes 8388632
  15.4 0.9 fusion
  16.5 8.1 %fusion.44 = bf16[32,128,128]{2,1,0:T(8,128)(2,1)} fusion(bf16[512,32,256]{0,2,1:T(8,128)(2,1)} %copy-done.2, f32[512]{0:T(512)S(1)} %convert_element_type.198, f32[512,32]{0,1:T(8,128)S(1)} %add_rsqrt_fusion.3, bf16[128,128]{1,0:T(8,128)(2,1)S(1)} %copy-done.7, f32[128]{0:T(128)S(1)} %add_rsqrt_fusion.10), kind=kOutput, calls=%fused_computation.49 | convolution fusion | flops 1086898176 | bytes 9538048 | tf_op jit(solution)/shard_map/fmr,rfe->fme/dot_general | solution.py:118
  24.6 7.2 %all-to-all-start = ((bf16[16,256,128]{2,1,0:T(8,128)(2,1)}), bf16[16,256,128]{2,1,0:T(8,128)(2,1)S(1)}, u32[]{:S(2)}, u32[]{:S(2)}) async-start(bf16[16,256,128]{2,1,0:T(8,128)(2,1)} %bitcast.4), calls=%async_computation | async-start | bytes 2097152 | tf_op jit(solution)/shard_map/all_to_all | solution.py:26
  31.8 0.2 fusion.71
  32.0 0.3 fusion.70
  32.3 17.2 %all-to-all-done = bf16[16,256,128]{2,1,0:T(8,128)(2,1)S(1)} async-done(((bf16[16,256,128]{2,1,0:T(8,128)(2,1)}), bf16[16,256,128]{2,1,0:T(8,128)(2,1)S(1)}, u32[]{:S(2)}, u32[]{:S(2)}) %all-to-all-start) | async-done | bytes 1048608 | tf_op jit(solution)/shard_map/all_to_all | solution.py:26
  49.5 0.8 reduce_sum.149
  50.3 7.6 %all-to-all-start.1 = ((bf16[4,64,128]{2,1,0:T(8,128)(2,1)}), bf16[4,64,128]{2,1,0:T(8,128)(2,1)S(1)}, u32[]{:S(2)}, u32[]{:S(2)}) async-start(bf16[4,64,128]{2,1,0:T(8,128)(2,1)} %bitcast.5), calls=%async_computation.1 | async-start | bytes 131072 | tf_op jit(solution)/shard_map/all_to_all | solution.py:26
  57.9 8.2 %all-to-all-done.1 = bf16[4,64,128]{2,1,0:T(8,128)(2,1)S(1)} async-done(((bf16[4,64,128]{2,1,0:T(8,128)(2,1)}), bf16[4,64,128]{2,1,0:T(8,128)(2,1)S(1)}, u32[]{:S(2)}, u32[]{:S(2)}) %all-to-all-start.1) | async-done | bytes 65568 | tf_op jit(solution)/shard_map/all_to_all | solution.py:26
  66.3 10.7 %all_to_all.40 = bf16[4,80,128]{2,1,0:T(8,128)(2,1)S(1)} all-to-all(bf16[4,80,128]{2,1,0:T(8,128)(2,1)S(1)} %broadcast_in_dim.18), channel_id=1, replica_groups=mesh['x'=4,'zh'=4,'y'=4,'zl'=2,'core'=2] {'zh'}, dimensions={0} | all-to-all | bytes 163840 | tf_op jit(solution)/shard_map/all_to_all | solution.py:26
  77.0 1.1 broadcast_in_dim.19
  78.2 3.7 %all-to-all-start.3 = ((bf16[16,272,128]{2,1,0:T(8,128)(2,1)}), bf16[16,272,128]{2,1,0:T(8,128)(2,1)S(1)}, u32[]{:S(2)}, u32[]{:S(2)}) async-start(bf16[16,272,128]{2,1,0:T(8,128)(2,1)} %broadcast_in_dim.19), calls=%async_computation.3 | async-start | bytes 2228224 | tf_op jit(solution)/shard_map/all_to_all | solution.py:26
  81.9 0.3 collective-permute-start
  82.3 5.5 %fusion.2 = (f32[512,32]{0,1:T(8,128)S(1)}, bf16[512,32,128]{0,2,1:T(8,128)(2,1)}) fusion(bf16[512,32,128]{0,2,1:T(8,128)(2,1)} %copy.101, bf16[128,384]{1,0:T(8,128)(2,1)S(1)} %copy-done.6), kind=kOutput, calls=%fused_computation.8 | convolution fusion | flops 545243136 | bytes 8486912 | tf_op jit(solution)/shard_map/rfe,ek->rfk/dot_general | solution.py:142
  87.8 7.4 %all-to-all-done.3 = bf16[16,272,128]{2,1,0:T(8,128)(2,1)S(1)} async-done(((bf16[16,272,128]{2,1,0:T(8,128)(2,1)}), bf16[16,272,128]{2,1,0:T(8,128)(2,1)S(1)}, u32[]{:S(2)}, u32[]{:S(2)}) %all-to-all-start.3) | async-done | bytes 1114144 | tf_op jit(solution)/shard_map/all_to_all | solution.py:26
  95.3 0.7 convolution_convert_fusion.3
  96.0 0.6 fusion.36
  96.6 0.8 copy-done.3
  97.4 4.4 %bitcast_reduce_fusion = (f32[512,32]{0,1:T(8,128)S(1)}, f32[32,128,512]{2,1,0:T(8,128)}) fusion(bf16[512,32,128]{0,2,1:T(8,128)(2,1)S(1)} %copy-done.3, f32[512,32]{0,1:T(8,128)S(1)} %add_rsqrt_fusion.2, f32[32,128]{1,0:T(8,128)S(1)} %add_rsqrt_fusion.4, bf16[32,128,256]{2,1,0:T(8,128)(2,1)S(1)} %convolution_convert_fusion.3), kind=kOutput, calls=%fused_computation.15 | convolution fusion | flops 548913152 | bytes 13778944 | tf_op jit(solution)/shard_map/rfe,fme->rfm/dot_general | solution.py:148
  101.8 9.6 %convolution_convert_fusion = bf16[512,32,256]{0,2,1:T(8,128)(2,1)} fusion(bf16[512,32,128]{0,2,1:T(8,128)(2,1)} %copy.101, f32[32,128,512]{2,1,0:T(8,128)} %get-tuple-element.16, f32[512,32]{0,1:T(8,128)S(1)} %get-tuple-element.15, bf16[32,128,256]{2,1,0:T(8,128)(2,1)S(1)} %convolution_convert_fusion.3, bf16[128,256]{1,0:T(8,128)(2,1)S(1)} %copy-done.10), kind=kOutput, calls=%fused_computation.19 | convolution fusion | flops 1627389952 | bytes 22151168 | tf_op jit(solution)/shard_map/rfe,ek->rfk/dot_general | solution.py:157
  111.4 4.9 %slice.86 = bf16[512,32,128]{0,2,1:T(8,128)(2,1)} slice(bf16[512,32,256]{0,2,1:T(8,128)(2,1)} %convolution_convert_fusion), slice={[0:512], [0:32], [128:256]} | slice | bytes 8388608 | tf_op jit(solution)/shard_map/slice | solution.py:168
  116.3 1.2 copy-done.4
  117.6 0.9 fusion.4
  118.5 8.0 %copy.116 = bf16[512,32,128]{2,1,0:T(8,128)(2,1)} copy(bf16[512,32,128]{0,2,1:T(8,128)(2,1)} %slice.86) | data formatting | bytes 8388608 | tf_op jit(solution)/shard_map/slice | solution.py:168
  126.6 3.1 %fusion.63 = bf16[512,32,4]{0,2,1:T(4,128)(2,1)S(1)} fusion(f32[512,32]{0,1:T(8,128)S(1)} %add_rsqrt_fusion.1, bf16[512,32,256]{0,2,1:T(8,128)(2,1)} %convolution_convert_fusion, bf16[4,128]{1,0:T(4,128)(2,1)S(1)} %copy-done.11, f32[4]{0:T(128)S(1)} %add_rsqrt_fusion.8), kind=kOutput, calls=%fused_computation.57 | convolution fusion | flops 23201280 | bytes 4391952 | tf_op jit(solution)/shard_map/ce,rfe->rcf/dot_general | solution.py:163
  129.6 0.3 copy.115
  130.0 3.4 %convolution_convert_fusion.5 = bf16[512,4,128]{2,1,0:T(4,128)(2,1)S(1)} fusion(bf16[512,32,4]{1,2,0:T(4,128)(2,1)S(1)} %copy.115, bf16[512,32,128]{2,1,0:T(8,128)(2,1)} %copy.116), kind=kOutput, calls=%fused_computation.51 | convolution fusion | flops 17039360 | bytes 4849664 | tf_op jit(solution)/shard_map/rcf,rfe->rce/dot_general | solution.py:167
  133.4 1.3 convolution_convert_fusion.4
  134.6 4.4 %all-to-all-start.4 = ((bf16[4,128,512]{2,1,0:T(8,128)(2,1)}), bf16[4,128,512]{2,1,0:T(8,128)(2,1)S(1)}, u32[]{:S(2)}, u32[]{:S(2)}) async-start(bf16[4,128,512]{2,1,0:T(8,128)(2,1)} %bitcast.17), calls=%async_computation.4 | async-start | bytes 1048576 | tf_op jit(solution)/shard_map/all_to_all | solution.py:26
  139.1 1.2 pad_maximum_fusion.2
  140.3 0.4 collective-permute-start.1
  140.6 5.8 %all-to-all-done.4 = bf16[4,128,512]{2,1,0:T(8,128)(2,1)S(1)} async-done(((bf16[4,128,512]{2,1,0:T(8,128)(2,1)}), bf16[4,128,512]{2,1,0:T(8,128)(2,1)S(1)}, u32[]{:S(2)}, u32[]{:S(2)}) %all-to-all-start.4) | async-done | bytes 524320 | tf_op jit(solution)/shard_map/all_to_all | solution.py:26
  146.7 0.2 reduce_sum.158
  146.9 16.3 %collective-permute-done.1 = bf16[3,512,256]{2,1,0:T(8,128)(2,1)} collective-permute-done((bf16[3,512,256]{2,1,0:T(8,128)(2,1)S(1)}, bf16[3,512,256]{2,1,0:T(8,128)(2,1)}, u32[]{:S(2)}, u32[]{:S(2)}) %collective-permute-start.1) | collective-permute-done | bytes 786464 | tf_op jit(solution)/shard_map/ppermute | solution.py:64
  163.2 0.2 mul.215
  163.4 1.7 fusion.54
  165.2 0.1 broadcast_select_fusion.2
  165.4 0.3 rev.21
  165.7 0.1 broadcast_select_fusion
  165.9 0.7 rev.19
  166.6 0.5 multiply_reduce_fusion.1
  167.1 0.1 copy.120
  167.3 0.2 multiply_convert_fusion.2
  167.5 0.9 broadcast_in_dim.20
  168.4 5.0 %all-to-all-start.5 = ((bf16[16,128,128]{2,1,0:T(8,128)(2,1)}), bf16[16,128,128]{2,1,0:T(8,128)(2,1)S(1)}, u32[]{:S(2)}, u32[]{:S(2)}) async-start(bf16[16,128,128]{2,1,0:T(8,128)(2,1)} %bitcast.23), calls=%async_computation.5 | async-start | bytes 1048576 | tf_op jit(solution)/shard_map/all_to_all | solution.py:26
  173.4 0.3 multiply_reduce_fusion.2
  173.9 0.3 rev.23
  174.3 0.1 multiply_convert_fusion.4
  174.5 13.1 %all-to-all-done.5 = bf16[16,128,128]{2,1,0:T(8,128)(2,1)S(1)} async-done(((bf16[16,128,128]{2,1,0:T(8,128)(2,1)}), bf16[16,128,128]{2,1,0:T(8,128)(2,1)S(1)}, u32[]{:S(2)}, u32[]{:S(2)}) %all-to-all-start.5) | async-done | bytes 524320 | tf_op jit(solution)/shard_map/all_to_all | solution.py:26
  187.6 1.9 broadcast_in_dim.23
  189.5 7.1 %all-to-all-start.6 = ((bf16[64,128,128]{2,1,0:T(8,128)(2,1)}), bf16[64,128,128]{2,1,0:T(8,128)(2,1)S(1)}, u32[]{:S(2)}, u32[]{:S(2)}) async-start(bf16[64,128,128]{2,1,0:T(8,128)(2,1)} %bitcast.95), calls=%async_computation.6 | async-start | bytes 4194304 | tf_op jit(solution)/shard_map/all_to_all | solution.py:26
  196.8 0.3 select_convert_fusion
  197.1 0.6 compare_convert_fusion
  197.7 2.1 pad_maximum_fusion.1.refs_0_
  199.9 24.9 %all-to-all-done.6 = bf16[64,128,128]{2,1,0:T(8,128)(2,1)S(1)} async-done(((bf16[64,128,128]{2,1,0:T(8,128)(2,1)}), bf16[64,128,128]{2,1,0:T(8,128)(2,1)S(1)}, u32[]{:S(2)}, u32[]{:S(2)}) %all-to-all-start.6) | async-done | bytes 2097184 | tf_op jit(solution)/shard_map/all_to_all | solution.py:26
  224.8 1.2 fusion.115
  225.9 1.6 pad_maximum_fusion.refs_1_
  227.5 13.7 %attention.1 = bf16[2048,128]{1,0:T(8,128)(2,1)} custom-call(bf16[2048,256]{1,0:T(8,128)(2,1)} %pad_maximum_fusion.1.refs_0_, bf16[4096,256]{1,0:T(8,128)(2,1)} %pad_maximum_fusion.refs_1_, bf16[4096,128]{1,0:T(8,128)(2,1)} %bitcast.97), custom_call_target="tpu_custom_call" | custom-call | tf_op jit(solution)/shard_map/attention/pallas_call | solution.py:49
  241.2 17.5 %all_to_all.41 = bf16[4,512,128]{2,1,0:T(8,128)(2,1)S(1)} all-to-all(bf16[4,512,128]{2,1,0:T(8,128)(2,1)} %bitcast.99), channel_id=1, replica_groups=mesh['x'=4,'zh'=4,'y'=4,'zl'=2,'core'=2] {'zh'}, dimensions={0} | all-to-all | bytes 1048576 | tf_op jit(solution)/shard_map/all_to_all | solution.py:26
  258.8 0.1 multiply_reduce_fusion
  258.9 1.2 convolution_convert_fusion.6
  (74 shorter events, 1.7 us)
Async XLA Ops:
  0.0 7.6 %copy-start = (bf16[128,256]{1,0:T(8,128)(2,1)S(1)}, bf16[128,256]{1,0:T(8,128)(2,1)}, u32[]{:S(2)}) copy-start(bf16[128,256]{1,0:T(8,128)(2,1)} %param.13) | copy-start | bytes 196612
  12.1 3.2 %copy-start.2 = (bf16[512,32,256]{0,2,1:T(8,128)(2,1)}, bf16[512,32,256]{0,2,1:T(8,128)(2,1)S(1)}, u32[]{:S(2)}) copy-start(bf16[512,32,256]{0,2,1:T(8,128)(2,1)S(1)} %convolution_convert_fusion.1) | copy-start | bytes 25165828
  15.4 1.0 copy-start.8
  15.4 1.0 copy-start.7
  16.5 15.3 %copy-start.9 = (s32[512]{0:T(512)S(1)}, s32[512]{0:T(512)}, u32[]{:S(2)}) copy-start(s32[512]{0:T(512)} %param.10) | copy-start | bytes 6148
  24.6 57.6 %copy-start.11 = (bf16[4,128]{1,0:T(4,128)(2,1)S(1)}, bf16[4,128]{1,0:T(4,128)(2,1)}, u32[]{:S(2)}) copy-start(bf16[4,128]{1,0:T(4,128)(2,1)} %param.15) | copy-start | bytes 3076
  24.6 57.7 %copy-start.6 = (bf16[128,384]{1,0:T(8,128)(2,1)S(1)}, bf16[128,384]{1,0:T(8,128)(2,1)}, u32[]{:S(2)}) copy-start(bf16[128,384]{1,0:T(8,128)(2,1)} %param.14) | copy-start | bytes 294916
  24.6 24.9 %all-to-all-start = ((bf16[16,256,128]{2,1,0:T(8,128)(2,1)}), bf16[16,256,128]{2,1,0:T(8,128)(2,1)S(1)}, u32[]{:S(2)}, u32[]{:S(2)}) async-start(bf16[16,256,128]{2,1,0:T(8,128)(2,1)} %bitcast.4), calls=%async_computation | async-start | bytes 2097152 | tf_op jit(solution)/shard_map/all_to_all | solution.py:26
  50.3 15.8 %all-to-all-start.1 = ((bf16[4,64,128]{2,1,0:T(8,128)(2,1)}), bf16[4,64,128]{2,1,0:T(8,128)(2,1)S(1)}, u32[]{:S(2)}, u32[]{:S(2)}) async-start(bf16[4,64,128]{2,1,0:T(8,128)(2,1)} %bitcast.5), calls=%async_computation.1 | async-start | bytes 131072 | tf_op jit(solution)/shard_map/all_to_all | solution.py:26
  78.2 17.0 %all-to-all-start.3 = ((bf16[16,272,128]{2,1,0:T(8,128)(2,1)}), bf16[16,272,128]{2,1,0:T(8,128)(2,1)S(1)}, u32[]{:S(2)}, u32[]{:S(2)}) async-start(bf16[16,272,128]{2,1,0:T(8,128)(2,1)} %broadcast_in_dim.19), calls=%async_computation.3 | async-start | bytes 2228224 | tf_op jit(solution)/shard_map/all_to_all | solution.py:26
  81.9 57.2 %collective-permute-start = (bf16[3,512,128]{2,1,0:T(8,128)(2,1)}, bf16[3,512,128]{2,1,0:T(8,128)(2,1)}, u32[]{:S(2)}, u32[]{:S(2)}) collective-permute-start(bf16[3,512,128]{2,1,0:T(8,128)(2,1)} %param.17), channel_id=1, source_target_pairs={{0,1},{1,0},{2,3},{3,2},{4,5},{5,4},{6,7},{7,6},{8,9},{9,8},{10,11... | collective-permute-start | bytes 1179656 | tf_op jit(solution)/shard_map/ppermute | solution.py:64
  95.2 2.2 copy-start.3
  97.4 4.4 %copy-start.10 = (bf16[128,256]{1,0:T(8,128)(2,1)S(1)}, bf16[128,256]{1,0:T(8,128)(2,1)}, u32[]{:S(2)}) copy-start(bf16[128,256]{1,0:T(8,128)(2,1)} %param.16) | copy-start | bytes 196612
  111.4 6.2 %copy-start.4 = (bf16[512,32,256]{0,2,1:T(8,128)(2,1)S(1)}, bf16[512,32,256]{0,2,1:T(8,128)(2,1)}, u32[]{:S(2)}) copy-start(bf16[512,32,256]{0,2,1:T(8,128)(2,1)} %convolution_convert_fusion) | copy-start | bytes 25165828
  134.6 11.8 %all-to-all-start.4 = ((bf16[4,128,512]{2,1,0:T(8,128)(2,1)}), bf16[4,128,512]{2,1,0:T(8,128)(2,1)S(1)}, u32[]{:S(2)}, u32[]{:S(2)}) async-start(bf16[4,128,512]{2,1,0:T(8,128)(2,1)} %bitcast.17), calls=%async_computation.4 | async-start | bytes 1048576 | tf_op jit(solution)/shard_map/all_to_all | solution.py:26
  140.3 22.9 %collective-permute-start.1 = (bf16[3,512,256]{2,1,0:T(8,128)(2,1)S(1)}, bf16[3,512,256]{2,1,0:T(8,128)(2,1)}, u32[]{:S(2)}, u32[]{:S(2)}) collective-permute-start(bf16[3,512,256]{2,1,0:T(8,128)(2,1)S(1)} %pad_maximum_fusion.2), channel_id=1, source_target_pairs={{0,2},{2,0},{1,3},{3,1},{4,6},{6,4},{5,7},{7,5},{8,10},{10,8},{9,1... | collective-permute-start | bytes 2359304 | tf_op jit(solution)/shard_map/ppermute | solution.py:64
  168.4 19.2 %all-to-all-start.5 = ((bf16[16,128,128]{2,1,0:T(8,128)(2,1)}), bf16[16,128,128]{2,1,0:T(8,128)(2,1)S(1)}, u32[]{:S(2)}, u32[]{:S(2)}) async-start(bf16[16,128,128]{2,1,0:T(8,128)(2,1)} %bitcast.23), calls=%async_computation.5 | async-start | bytes 1048576 | tf_op jit(solution)/shard_map/all_to_all | solution.py:26
  187.6 1.9 copy-start.5
  189.5 35.3 %all-to-all-start.6 = ((bf16[64,128,128]{2,1,0:T(8,128)(2,1)}), bf16[64,128,128]{2,1,0:T(8,128)(2,1)S(1)}, u32[]{:S(2)}, u32[]{:S(2)}) async-start(bf16[64,128,128]{2,1,0:T(8,128)(2,1)} %bitcast.95), calls=%async_computation.6 | async-start | bytes 4194304 | tf_op jit(solution)/shard_map/all_to_all | solution.py:26
  225.9 34.2 %copy-start.1 = (bf16[128,256]{1,0:T(8,128)(2,1)S(1)}, bf16[128,256]{1,0:T(8,128)(2,1)}, u32[]{:S(2)}) copy-start(bf16[128,256]{1,0:T(8,128)(2,1)} %param.13) | copy-start | bytes 196612

commit v2 on v1

v2 whole, which is shorter than its diff:
```python
import jax
import jax.numpy as jnp
from jax import lax
from jax.experimental import pallas as pl
from jax.experimental.pallas import tpu as pltpu
from jax.sharding import Mesh, PartitionSpec as P

HEAD_DIM = 128
XY = ("x", "y")
FEAT = ("zl", "core")
KEY_GROUP = ("x", "y", "zl", "core")
QUERY_GROUP = ("zh", "zl", "core")
FOLD_PENALTY = 16384.0

epsilon = 1e-06
score_scale = 0.25
LOG2E = 1.4426950408889634
EXCLUDED = -1e9


def rms_normalize(value):
    value = value.astype(jnp.float32)
    return value * lax.rsqrt(jnp.mean(value * value, axis=-1, keepdims=True) + epsilon)


def product(a, b):
    return jnp.dot(a, b, preferred_element_type=jnp.float32)


def product_nt(a, b):
    return lax.dot_general(a, b, (((1,), (1,)), ((), ())), preferred_element_type=jnp.float32)


def induce_kernel(x_ref, bias_ref, proj_ref, points_ref, cells_ref, sums_ref, stage_ref):
    chunk, feats, embed = x_ref.shape
    step = pl.program_id(0)
    stage_ref[...] = x_ref[...].astype(jnp.float32).reshape(chunk * feats, embed)
    first = pl.multiple_of(step * chunk, chunk)
    for f in range(feats):
        cells_ref[f, pl.ds(first, chunk), :] = stage_ref[
            pl.ds(f, chunk, stride=feats), :
        ].astype(jnp.bfloat16)

    @pl.when(step == pl.num_programs(0) - 1)
    def _():
        points = points_ref[...]
        ones = jnp.ones((8, embed), jnp.bfloat16)
        bias = bias_ref[0:1, :]

        def feature(f, carry):
            kv = product(cells_ref[f], proj_ref[...]).astype(jnp.bfloat16)
            keys = kv[:, :embed]
            wide = keys.astype(jnp.float32)
            squares = product_nt(ones, (wide * wide).astype(jnp.bfloat16))
            factor = lax.rsqrt(squares * (1.0 / embed) + epsilon) * (score_scale * LOG2E)
            scores = product_nt(points, keys) * factor[0:1, :] + bias
            weights = jnp.exp2(scores).astype(jnp.bfloat16)
            sums_ref[f] = product(weights, kv[:, embed:]).astype(jnp.bfloat16)
            return carry

        lax.fori_loop(0, feats, feature, 0, unroll=4)


def induce(table_cells, bias, induce_proj, induce_norm, chunk=64):
    rows, feats, embed = table_cells.shape
    points = induce_norm.shape[0]
    return pl.pallas_call(
        induce_kernel,
        out_shape=(
            jax.ShapeDtypeStruct((feats, rows, embed), jnp.bfloat16),
            jax.ShapeDtypeStruct((feats, points, embed), jnp.bfloat16),
        ),
        grid=(rows // chunk,),
        in_specs=[
            pl.BlockSpec((chunk, feats, embed), lambda i: (i, 0, 0)),
            pl.BlockSpec(bias.shape, lambda i: (0, 0)),
            pl.BlockSpec(induce_proj.shape, lambda i: (0, 0)),
            pl.BlockSpec(induce_norm.shape, lambda i: (0, 0)),
        ],
        out_specs=(
            pl.BlockSpec((feats, rows, embed), lambda i: (0, 0, 0)),
            pl.BlockSpec((feats, points, embed), lambda i: (0, 0, 0)),
        ),
        scratch_shapes=[pltpu.VMEM((chunk * feats, embed), jnp.float32)],
        name="induce",
    )(table_cells, bias, induce_proj, induce_norm)


def cell_query_kernel(x_ref, proj_ref, o_ref):
    feats, rows, embed = x_ref.shape
    query = product(x_ref[...].reshape(feats * rows, embed), proj_ref[...]).astype(jnp.bfloat16)
    o_ref[...] = rms_normalize(query).astype(jnp.bfloat16).reshape(o_ref.shape)


def cell_queries(cells, proj, step=4):
    feats, rows, embed = cells.shape
    return pl.pallas_call(
        cell_query_kernel,
        out_shape=jax.ShapeDtypeStruct(cells.shape, jnp.bfloat16),
        grid=(feats // step,),
        in_specs=[
            pl.BlockSpec((step, rows, embed), lambda i: (i, 0, 0)),
            pl.BlockSpec(proj.shape, lambda i: (0, 0)),
        ],
        out_specs=pl.BlockSpec((step, rows, embed), lambda i: (i, 0, 0)),
        name="cell_queries",
    )(cells, proj)


def summary_kernel(
    induced_ref, cells_ref, query_ref, back_ref, row_ref, summary_ref, permute_ref, o_ref, total_ref
):
    step = pl.program_id(0)
    feats, rows, embed = cells_ref.shape
    points = embed
    summaries = total_ref.shape[1] // embed
    back = back_ref[...]
    row_proj = row_ref[...]
    summary = summary_ref[...]
    ones = jnp.ones((points, embed), jnp.bfloat16)
    parts = []
    for f in range(feats):
        induced = induced_ref[0, f * points : (f + 1) * points, :]
        point_kv = product(induced, back).astype(jnp.bfloat16)
        point_keys = (rms_normalize(point_kv[:, :embed]) * (score_scale * LOG2E)).astype(
            jnp.bfloat16
        )
        expos = jnp.exp2(product_nt(query_ref[f], point_keys)).astype(jnp.bfloat16)
        mixed = product(expos, jnp.concatenate([point_kv[:, embed:], ones], axis=1))
        attended = mixed[:, :embed] / mixed[:, embed:]
        updated = (cells_ref[f].astype(jnp.float32) + attended).astype(jnp.bfloat16)
        row_kv = product(updated, row_proj).astype(jnp.bfloat16)
        keys = row_kv[:, :embed]
        wide = keys.astype(jnp.float32)
        factor = lax.rsqrt(jnp.mean(wide * wide, axis=-1, keepdims=True) + epsilon)
        weights = jnp.exp2(product(keys, summary) * (factor * (score_scale * LOG2E)))
        parts.append(
            (weights.astype(jnp.bfloat16).astype(jnp.float32), row_kv[:, embed:].astype(jnp.float32))
        )
    for c in range(summaries):
        addend = parts[0][0][:, c : c + 1] * parts[0][1]
        for weights, values in parts[1:]:
            addend = addend + weights[:, c : c + 1] * values
        span = slice(c * embed, (c + 1) * embed)

        @pl.when(step == 0)
        def _():
            total_ref[:, span] = addend

        @pl.when(step > 0)
        def _():
            total_ref[:, span] += addend

    @pl.when(step == pl.num_programs(0) - 1)
    def _():
        o_ref[...] = product(permute_ref[...], total_ref[...].astype(jnp.bfloat16)).astype(
            jnp.bfloat16
        )


def summarize(induced, cells, queries, back, row_proj, summary, permute, summaries, step=2):
    feats, rows, embed = cells.shape
    width = summaries * embed
    return pl.pallas_call(
        summary_kernel,
        out_shape=jax.ShapeDtypeStruct((rows, width), jnp.bfloat16),
        grid=(feats // step,),
        in_specs=[
            pl.BlockSpec((1,) + induced.shape[1:], lambda i: (i, 0, 0)),
            pl.BlockSpec((step, rows, embed), lambda i: (i, 0, 0)),
            pl.BlockSpec((step, rows, embed), lambda i: (i, 0, 0)),
            pl.BlockSpec(back.shape, lambda i: (0, 0)),
            pl.BlockSpec(row_proj.shape, lambda i: (0, 0)),
            pl.BlockSpec(summary.shape, lambda i: (0, 0)),
            pl.BlockSpec(permute.shape, lambda i: (0, 0)),
        ],
        out_specs=pl.BlockSpec((rows, width), lambda i: (0, 0)),
        scratch_shapes=[pltpu.VMEM((rows, width), jnp.float32)],
        name="summarize",
    )(induced, cells, queries, back, row_proj, summary, permute)


def attention_kernel(q_ref, qm_ref, kv_ref, km_ref, o_ref, *, groups):
    q = jnp.concatenate([q_ref[...], qm_ref[...]], axis=1)
    count, both, dim = kv_ref.shape
    half = both // 2
    total = jnp.zeros(o_ref.shape, jnp.float32)
    for g in range(0, count, groups):
        k = jnp.concatenate(
            [
                kv_ref[g : g + groups, :half, :].reshape(groups * half, dim),
                km_ref[g * half : (g + groups) * half, :],
            ],
            axis=1,
        )
        v = kv_ref[g : g + groups, half:, :].reshape(groups * half, dim)
        weights = jnp.exp2(product_nt(q, k)).astype(jnp.bfloat16)
        total = total + product(weights, v)
    o_ref[...] = total.astype(o_ref.dtype)


def attention(q, q_marks, kv, k_marks, query_block=512, groups=8):
    queries, dim = q.shape
    return pl.pallas_call(
        lambda *refs: attention_kernel(*refs, groups=groups),
        out_shape=jax.ShapeDtypeStruct((queries, dim), jnp.bfloat16),
        grid=(queries // query_block,),
        in_specs=[
            pl.BlockSpec((query_block, dim), lambda i: (i, 0)),
            pl.BlockSpec((query_block, dim), lambda i: (i, 0)),
            pl.BlockSpec(kv.shape, lambda i: (0, 0, 0)),
            pl.BlockSpec(k_marks.shape, lambda i: (0, 0)),
        ],
        out_specs=pl.BlockSpec((query_block, dim), lambda i: (i, 0)),
        name="attention",
    )(q, q_marks, kv, k_marks)

def exchange(value, axes):
    return lax.all_to_all(value, axes, 0, 0, tiled=True)


def other(value, axis):
    return lax.ppermute(value, axis, [(0, 1), (1, 0)])


def local(
    table_cells,
    fold_id,
    train_mask,
    inducing,
    induce_proj,
    induce_back,
    summary_query,
    row_proj,
    context_proj,
):
    rows_here, feats_here, embed = table_cells.shape
    width = context_proj.shape[1]
    zl = lax.axis_index("zl")
    core = lax.axis_index("core")
    zh = lax.axis_index("zh")
    xy = lax.axis_index("x") * lax.axis_size("y") + lax.axis_index("y")
    groups_xy = lax.axis_size("x") * lax.axis_size("y")
    groups_z = lax.axis_size("zh")
    feat_devices = lax.axis_size("zl") * lax.axis_size("core")
    block = rows_here // feat_devices
    half = block // 2

    proj_pair = jnp.concatenate([context_proj, other(context_proj, "core")], axis=2)
    proj_full = jnp.concatenate([proj_pair, other(proj_pair, "zl")], axis=2)

    labelled = (train_mask == 1).astype(jnp.bfloat16)
    index = jnp.arange(rows_here)
    before = (index[:, None] < index[None, :]).astype(jnp.bfloat16)
    rank_train = jnp.dot(labelled[None], before, preferred_element_type=jnp.float32)[0].astype(
        jnp.int32
    )
    rank = jnp.where(train_mask == 1, rank_train, index - rank_train)
    slot = (rank // half) * block + rank % half + jnp.where(train_mask == 1, 0, half)
    permute = (index[:, None] == slot[None, :]).astype(jnp.bfloat16)
    codes = jnp.dot(
        permute, fold_id.astype(jnp.bfloat16)[:, None], preferred_element_type=jnp.float32
    ).astype(jnp.bfloat16)
    codes = codes.reshape(feat_devices, block)

    induce_norm = rms_normalize(inducing).astype(jnp.bfloat16)
    bias = jnp.broadcast_to(
        jnp.where(train_mask == 1, 0.0, EXCLUDED)[None], (8, rows_here)
    ).astype(jnp.float32)
    cells, numerator = induce(table_cells, bias, induce_proj, induce_norm)
    points = inducing.shape[0]
    share_xy = feats_here * points // groups_xy
    part = exchange(numerator.reshape(groups_xy, share_xy, embed), XY)
    part, proj_full = lax.optimization_barrier((part, proj_full))
    part = jnp.sum(part.astype(jnp.float32), axis=0).astype(jnp.bfloat16)
    queries = cell_queries(cells, induce_back[:, :embed])
    sent = jnp.concatenate([part, jnp.pad(codes, ((0, 12), (0, 0)))], axis=0)
    got = exchange(jnp.broadcast_to(sent[None], (groups_z,) + sent.shape), "zh")
    mine = rms_normalize(jnp.sum(got[:, :share_xy].astype(jnp.float32), axis=0))
    sent = jnp.concatenate(
        [mine.astype(jnp.bfloat16), got[:, share_xy : share_xy + 4].reshape(-1, embed)], axis=0
    )
    got = exchange(jnp.broadcast_to(sent[None], (groups_xy,) + sent.shape), XY)
    all_codes = got[:, share_xy:].reshape(groups_xy, groups_z, feat_devices, block)

    summary = rms_normalize(summary_query).astype(jnp.bfloat16).T
    summaries = summary.shape[1]
    summary = jnp.pad(summary, ((0, 0), (0, embed - summaries)))
    ordered = summarize(
        got, cells, queries, induce_back[:, embed:], row_proj, summary, permute, summaries
    )
    got = exchange(ordered.reshape(feat_devices, block, width), FEAT)
    totals = jnp.sum(got.astype(jnp.float32), axis=0)
    represent = rms_normalize(totals.reshape(block, -1, embed)).astype(jnp.bfloat16)
    projected = jnp.einsum(
        "rd,kdc->krc",
        represent.reshape(block, width),
        proj_full,
        preferred_element_type=jnp.float32,
    ).astype(jnp.bfloat16)

    def heads(value):
        value = value.reshape(-1, 2, 2, HEAD_DIM).transpose(1, 2, 0, 3)
        value = jnp.where(zl == 0, value, value[::-1])
        return jnp.where(core == 0, value, value[:, ::-1]).reshape(
            feat_devices, -1, HEAD_DIM
        )

    q = (rms_normalize(heads(projected[0])) * (score_scale * LOG2E)).astype(jnp.bfloat16)
    k = rms_normalize(heads(projected[1][:half])).astype(jnp.bfloat16)
    v = heads(projected[2][:half])
    q_all = exchange(
        jnp.broadcast_to(q[None], (groups_z,) + q.shape).reshape(-1, block, HEAD_DIM), QUERY_GROUP
    ).reshape(-1, HEAD_DIM)
    kv = jnp.concatenate([k, v], axis=1)
    kv_all = exchange(
        jnp.broadcast_to(kv[None], (groups_xy,) + kv.shape).reshape(-1, 2 * half, HEAD_DIM),
        KEY_GROUP,
    )
    query_codes = lax.dynamic_index_in_dim(all_codes, xy, 0, keepdims=False).reshape(-1)
    key_codes = lax.dynamic_index_in_dim(all_codes, zh, 1, keepdims=False)[..., :half].reshape(-1)
    lanes = jnp.arange(HEAD_DIM).astype(jnp.float32)
    query_marks = jnp.where(
        query_codes.astype(jnp.float32)[:, None] == lanes[None], -FOLD_PENALTY, 0.0
    ).astype(jnp.bfloat16)
    key_marks = (key_codes.astype(jnp.float32)[:, None] == lanes[None]).astype(jnp.bfloat16)
    summed = attention(q_all, query_marks, kv_all, key_marks)
    got = exchange(summed.reshape(groups_z, rows_here, HEAD_DIM), "zh")
    context = rms_normalize(jnp.sum(got.astype(jnp.float32), axis=0)).astype(jnp.bfloat16)
    return lax.dot_general(
        permute, context, (((0,), (0,)), ((), ())), preferred_element_type=jnp.float32
    ).astype(jnp.bfloat16)


def solution(mesh):
    fine = Mesh(mesh.devices.reshape(4, 4, 4, 2, 2), ("x", "zh", "y", "zl", "core"))
    rows = ("x", "zh", "y")
    in_specs = (
        P(rows, FEAT, None),
        P(rows),
        P(rows),
        P(),
        P(),
        P(),
        P(),
        P(),
        P(None, None, FEAT),
    )
    return jax.shard_map(
        local, mesh=fine, in_specs=in_specs, out_specs=P(rows, FEAT), check_vma=False
    )
```

time: 265 us -> 249 us (0.940)
  Pallas kernels: 13.7 us -> 85.2 us
  matrix products: 43.9 us -> 2.05 us
  waiting for transfers between devices: 93 us -> 67.6 us
  local copies, waits for them, and re-layouts: 33.5 us -> 12.2 us
  blocking collectives: 28.2 us -> 36.1 us
  starting transfers between devices: 35.6 us -> 30.8 us
    pallas_call x1 -> x4, Pallas kernels: 13.7 us -> 85.2 us  [the longest x1 37.4 us: summarize(): pl.pallas_call(summary_kernel, out_shape=jax.ShapeDtypeStruct((rows, widt...]
    dot_general x9 -> x0, matrix products: 40.5 us -> none  [the longest x1 9.61 us: local(): jnp.einsum('rfe,ek->rfk', updated, row_proj, preferred_element_type=jnp.f...]
    all_to_all x6 -> x5, waiting for transfers between devices: 76.7 us -> 48.5 us  [exchange(): return lax.all_to_all(value, axes, 0, 0, tiled=True)]
    slice x6 -> x3, local copies, waits for them, and re-layouts: 14.2 us -> 1.24 us  [the longest x1 0.63 us: local(): induce_back[:, embed:]]
    unnamed x25 -> x14, local copies, waits for them, and re-layouts: 12.8 us -> 2.46 us
    all_to_all x2, blocking collectives: 28.2 us -> 36.1 us  [exchange(): return lax.all_to_all(value, axes, 0, 0, tiled=True)]
    all_to_all x6 -> x5, starting transfers between devices: 35 us -> 30.7 us  [exchange(): return lax.all_to_all(value, axes, 0, 0, tiled=True)]
    concatenate x4 -> x3, other arithmetic: 3.74 us -> 0.17 us  [the longest x1 0.15 us: local(): proj_full = jnp.concatenate([proj_pair, other(proj_pair, 'zl')], axis=2)]
  transfers between devices with their start and end apart: 8 -> 7, of which waited for: 7 -> 5; matrix products, arithmetic and copies ran while one was open for 19% -> 5% of each run, Pallas kernels for 0% -> 14%
where the time goes in v2:
time: 249 us; the launch traced here: 244 us
  Pallas kernels  85.2 us (34%)
  waiting for transfers between devices  67.6 us (27%)
  blocking collectives  36.1 us (14%)
  starting transfers between devices  30.8 us (12%)
  local copies, waits for them, and re-layouts  12.2 us (5%)
  other arithmetic  9.69 us (4%)
    all_to_all x5, waiting for transfers between devices, exchange(): return lax.all_to_all(value, axes, 0, 0, tiled=True)  48.5 us
    pallas_call x1, Pallas kernels, summarize(): pl.pallas_call(summary_kernel, out_shape=jax.ShapeDtypeStruct((rows, widt...  37.4 us
    all_to_all x2, blocking collectives, exchange(): return lax.all_to_all(value, axes, 0, 0, tiled=True)  36.1 us
    all_to_all x5, starting transfers between devices, exchange(): return lax.all_to_all(value, axes, 0, 0, tiled=True)  30.7 us
    pallas_call x1, Pallas kernels, induce(): pl.pallas_call(induce_kernel, out_shape=(jax.ShapeDtypeStruct((feats, row...  25.7 us
    ppermute x2, waiting for transfers between devices, other(): return lax.ppermute(value, axis, [(0, 1), (1, 0)])  19.1 us
    pallas_call x1, Pallas kernels, attention(): pl.pallas_call(lambda *refs: attention_kernel(*refs, groups=groups), out_...  13.8 us
    pallas_call x1, Pallas kernels, cell_queries(): pl.pallas_call(cell_query_kernel, out_shape=jax.ShapeDtypeStruct(cells.sh...  8.27 us
  transfers between devices with their start and end apart: 7, of which 5 were waited for; matrix products, arithmetic and copies ran while one was open for 5% of the time, Pallas kernels for 14%

profile of v2, /device:TPU:32, one launch (start us, length us, event | category | flops | bytes accessed | tf_op | source)
XLA Modules:
  0.0 244.0 jit_solution(13601733635348834085)
XLA Ops:
  0.0 0.7 broadcast_select_fusion.6
  0.7 0.9 fusion.13
  1.6 1.5 fusion.14.points_ref
  3.0 0.6 broadcast_in_dim.30.bias_ref
  3.6 25.7 %induce.1 = (bf16[32,512,128]{2,1,0:T(8,128)(2,1)}, bf16[32,128,128]{2,1,0:T(8,128)(2,1)}) custom-call(bf16[512,32,128]{2,1,0:T(8,128)(2,1)} %x_ref.1, f32[8,512]{1,0:T(8,128)} %broadcast_in_dim.30.bias_ref, bf16[128,256]{1,0:T(8,128)(2,1)} %proj_ref.1, bf16[128,128]{1,0:T(8,128)(2,1)} %fusion.14.points_ref), custom_call_target="tpu_custom_call" | custom-call | tf_op jit(solution)/shard_map/induce/pallas_call | solution.py:67
  29.4 7.2 %all-to-all-start = ((bf16[16,256,128]{2,1,0:T(8,128)(2,1)}), bf16[16,256,128]{2,1,0:T(8,128)(2,1)S(1)}, u32[]{:S(2)}, u32[]{:S(2)}) async-start(bf16[16,256,128]{2,1,0:T(8,128)(2,1)} %bitcast.49), calls=%async_computation | async-start | bytes 2097152 | tf_op jit(solution)/shard_map/all_to_all | solution.py:219
  36.6 0.1 pad_maximum_fusion.1
  36.7 0.2 collective-permute-start.1
  36.9 0.2 fusion.3
  37.1 0.3 fusion.2
  37.4 19.1 %collective-permute-done.1 = bf16[3,512,256]{2,1,0:T(8,128)(2,1)S(1)} collective-permute-done((bf16[3,512,256]{2,1,0:T(8,128)(2,1)S(1)}, bf16[3,512,256]{2,1,0:T(8,128)(2,1)S(1)}, u32[]{:S(2)}, u32[]{:S(2)}) %collective-permute-start.1) | collective-permute-done | bytes 786464 | tf_op jit(solution)/shard_map/ppermute | solution.py:223
  56.5 0.2 pad_maximum_fusion
  56.7 0.1 reduce_sum.103
  56.9 18.6 %all_to_all.35 = bf16[4,272,128]{2,1,0:T(8,128)(2,1)S(1)} all-to-all(bf16[4,272,128]{2,1,0:T(8,128)(2,1)S(1)} %broadcast_in_dim.31), channel_id=1, replica_groups=mesh['x'=4,'zh'=4,'y'=4,'zl'=2,'core'=2] {'zh'}, dimensions={0} | all-to-all | bytes 557056 | tf_op jit(solution)/shard_map/all_to_all | solution.py:219
  75.5 0.1 multiply_reduce_fusion.3
  75.6 0.1 multiply_convert_fusion.4
  75.8 1.2 broadcast_in_dim.32
  77.0 6.2 %all-to-all-start.2 = ((bf16[16,272,128]{2,1,0:T(8,128)(2,1)}), bf16[16,272,128]{2,1,0:T(8,128)(2,1)S(1)}, u32[]{:S(2)}, u32[]{:S(2)}) async-start(bf16[16,272,128]{2,1,0:T(8,128)(2,1)} %broadcast_in_dim.32), calls=%async_computation.2 | async-start | bytes 2228224 | tf_op jit(solution)/shard_map/all_to_all | solution.py:219
  83.3 0.6 slice.35.proj_ref
  83.9 0.6 slice.36.back_ref
  84.5 0.1 fusion.16
  84.7 0.1 copy.58
  84.9 0.6 pad.9.summary_ref
  85.5 8.3 %cell_queries.1.query_ref = bf16[32,512,128]{2,1,0:T(8,128)(2,1)} custom-call(bf16[32,512,128]{2,1,0:T(8,128)(2,1)} %get-tuple-element.12.x_ref.cells_ref, bf16[128,128]{1,0:T(8,128)(2,1)} %slice.35.proj_ref), custom_call_target="tpu_custom_call" | custom-call | tf_op jit(solution)/shard_map/cell_queries/pallas_call | solution.py:97
  93.8 0.9 fusion.1.permute_ref
  94.7 4.3 %all-to-all-done.2.induced_ref = bf16[16,272,128]{2,1,0:T(8,128)(2,1)S(1)} async-done(((bf16[16,272,128]{2,1,0:T(8,128)(2,1)}), bf16[16,272,128]{2,1,0:T(8,128)(2,1)S(1)}, u32[]{:S(2)}, u32[]{:S(2)}) %all-to-all-start.2) | async-done | bytes 1114144 | tf_op jit(solution)/shard_map/all_to_all | solution.py:219
  98.9 1.1 copy-done.1
  100.0 37.4 %summarize.1 = bf16[512,512]{1,0:T(8,128)(2,1)} custom-call(bf16[16,272,128]{2,1,0:T(8,128)(2,1)} %copy-done.1, bf16[32,512,128]{2,1,0:T(8,128)(2,1)} %get-tuple-element.12.x_ref.cells_ref, bf16[32,512,128]{2,1,0:T(8,128)(2,1)} %cell_queries.1.query_ref, bf16[128,256]{1,0:T(8,128)(2,1)} %slice.36.back_ref, bf16[128,256]{1,0:T(8,128)(2,1)} %row_ref.1, ...), custom_call_target="tpu_custom_call" | custom-call | tf_op jit(solution)/shard_map/summarize/pallas_call | solution.py:164
  137.5 3.7 %all-to-all-start.3 = ((bf16[4,128,512]{2,1,0:T(8,128)(2,1)}), bf16[4,128,512]{2,1,0:T(8,128)(2,1)S(1)}, u32[]{:S(2)}, u32[]{:S(2)}) async-start(bf16[4,128,512]{2,1,0:T(8,128)(2,1)} %bitcast.44), calls=%async_computation.3 | async-start | bytes 1048576 | tf_op jit(solution)/shard_map/all_to_all | solution.py:219
  141.2 7.2 %all-to-all-done.3 = bf16[4,128,512]{2,1,0:T(8,128)(2,1)S(1)} async-done(((bf16[4,128,512]{2,1,0:T(8,128)(2,1)}), bf16[4,128,512]{2,1,0:T(8,128)(2,1)S(1)}, u32[]{:S(2)}, u32[]{:S(2)}) %all-to-all-start.3) | async-done | bytes 524320 | tf_op jit(solution)/shard_map/all_to_all | solution.py:219
  148.5 0.1 mul.120
  148.6 0.2 reduce_sum.108
  148.8 0.2 mul.121
  149.0 0.4 fusion
  149.5 0.1 broadcast_select_fusion
  149.6 0.7 rev.19
  150.3 0.5 multiply_reduce_fusion.1
  150.8 0.1 copy.61
  150.9 0.1 copy.62
  151.0 0.2 multiply_convert_fusion.1
  151.3 0.9 broadcast_in_dim.33
  152.2 6.7 %all-to-all-start.4 = ((bf16[16,128,128]{2,1,0:T(8,128)(2,1)}), bf16[16,128,128]{2,1,0:T(8,128)(2,1)S(1)}, u32[]{:S(2)}, u32[]{:S(2)}) async-start(bf16[16,128,128]{2,1,0:T(8,128)(2,1)} %bitcast.12), calls=%async_computation.4 | async-start | bytes 1048576 | tf_op jit(solution)/shard_map/all_to_all | solution.py:219
  158.9 0.1 broadcast_select_fusion.2
  159.1 0.3 rev.23
  159.4 0.3 rev.21
  159.6 0.3 multiply_reduce_fusion.2
  159.9 0.1 copy.64
  160.0 0.1 copy.65
  160.1 0.1 broadcast_select_fusion.4
  160.2 0.1 multiply_convert_fusion.3
  160.3 0.1 pad_maximum_fusion.2
  160.5 12.6 %all-to-all-done.4 = bf16[16,128,128]{2,1,0:T(8,128)(2,1)S(1)} async-done(((bf16[16,128,128]{2,1,0:T(8,128)(2,1)}), bf16[16,128,128]{2,1,0:T(8,128)(2,1)S(1)}, u32[]{:S(2)}, u32[]{:S(2)}) %all-to-all-start.4) | async-done | bytes 524320 | tf_op jit(solution)/shard_map/all_to_all | solution.py:219
  173.1 1.9 broadcast_in_dim.36
  175.0 6.8 %all-to-all-start.5 = ((bf16[64,128,128]{2,1,0:T(8,128)(2,1)}), bf16[64,128,128]{2,1,0:T(8,128)(2,1)S(1)}, u32[]{:S(2)}, u32[]{:S(2)}) async-start(bf16[64,128,128]{2,1,0:T(8,128)(2,1)} %bitcast.41), calls=%async_computation.5 | async-start | bytes 4194304 | tf_op jit(solution)/shard_map/all_to_all | solution.py:219
  181.8 0.9 slice.45
  182.7 0.1 reshape.182
  182.8 1.1 select_convert_fusion.refs_1_
  184.0 1.6 compare_convert_fusion.refs_3_
  185.6 24.4 %all-to-all-done.5.refs_2_ = bf16[64,128,128]{2,1,0:T(8,128)(2,1)S(1)} async-done(((bf16[64,128,128]{2,1,0:T(8,128)(2,1)}), bf16[64,128,128]{2,1,0:T(8,128)(2,1)S(1)}, u32[]{:S(2)}, u32[]{:S(2)}) %all-to-all-start.5) | async-done | bytes 2097184 | tf_op jit(solution)/shard_map/all_to_all | solution.py:219
  210.0 1.3 copy-done
  211.3 13.8 %attention.1 = bf16[2048,128]{1,0:T(8,128)(2,1)} custom-call(bf16[2048,128]{1,0:T(8,128)(2,1)} %bitcast.42, bf16[2048,128]{1,0:T(8,128)(2,1)} %select_convert_fusion.refs_1_, bf16[64,128,128]{2,1,0:T(8,128)(2,1)} %copy-done, bf16[4096,128]{1,0:T(8,128)(2,1)} %compare_convert_fusion.refs_3_), custom_call_target="tpu_custom_call" | custom-call | tf_op jit(solution)/shard_map/attention/pallas_call | solution.py:204
  225.1 17.5 %all_to_all.36 = bf16[4,512,128]{2,1,0:T(8,128)(2,1)S(1)} all-to-all(bf16[4,512,128]{2,1,0:T(8,128)(2,1)} %bitcast.43), channel_id=1, replica_groups=mesh['x'=4,'zh'=4,'y'=4,'zl'=2,'core'=2] {'zh'}, dimensions={0} | all-to-all | bytes 1048576 | tf_op jit(solution)/shard_map/all_to_all | solution.py:219
  242.7 0.1 multiply_reduce_fusion
  242.8 1.2 convolution_convert_fusion.1
  (48 shorter events, 0.7 us)
Async XLA Ops:
  0.0 36.6 %collective-permute-start = (bf16[3,512,128]{2,1,0:T(8,128)(2,1)}, bf16[3,512,128]{2,1,0:T(8,128)(2,1)S(1)}, u32[]{:S(2)}, u32[]{:S(2)}) collective-permute-start(bf16[3,512,128]{2,1,0:T(8,128)(2,1)} %param.17), channel_id=1, source_target_pairs={{0,1},{1,0},{2,3},{3,2},{4,5},{5,4},{6,7},{7,6},{8,9},{9,8},{10,11... | collective-permute-start | bytes 1179656 | tf_op jit(solution)/shard_map/ppermute | solution.py:223
  29.4 7.2 %copy-start.5 = (s32[512]{0:T(512)S(1)}, s32[512]{0:T(512)}, u32[]{:S(2)}) copy-start(s32[512]{0:T(512)} %param.10) | copy-start | bytes 6148
  29.4 7.2 %copy-start.3 = (bf16[3,512,128]{2,1,0:T(8,128)(2,1)S(1)}, bf16[3,512,128]{2,1,0:T(8,128)(2,1)}, u32[]{:S(2)}) copy-start(bf16[3,512,128]{2,1,0:T(8,128)(2,1)} %param.17) | copy-start | bytes 1179652
  29.4 27.3 %all-to-all-start = ((bf16[16,256,128]{2,1,0:T(8,128)(2,1)}), bf16[16,256,128]{2,1,0:T(8,128)(2,1)S(1)}, u32[]{:S(2)}, u32[]{:S(2)}) async-start(bf16[16,256,128]{2,1,0:T(8,128)(2,1)} %bitcast.49), calls=%async_computation | async-start | bytes 2097152 | tf_op jit(solution)/shard_map/all_to_all | solution.py:219
  36.7 19.7 %collective-permute-start.1 = (bf16[3,512,256]{2,1,0:T(8,128)(2,1)S(1)}, bf16[3,512,256]{2,1,0:T(8,128)(2,1)S(1)}, u32[]{:S(2)}, u32[]{:S(2)}) collective-permute-start(bf16[3,512,256]{2,1,0:T(8,128)(2,1)S(1)} %pad_maximum_fusion.1), channel_id=1, source_target_pairs={{0,2},{2,0},{1,3},{3,1},{4,6},{6,4},{5,7},{7,5},{8,10},{10,8},{9,1... | collective-permute-start | bytes 2359304 | tf_op jit(solution)/shard_map/ppermute | solution.py:223
  75.8 7.5 %copy-start.4 = (bf16[128,384]{1,0:T(8,128)(2,1)S(1)}, bf16[128,384]{1,0:T(8,128)(2,1)}, u32[]{:S(2)}) copy-start(bf16[128,384]{1,0:T(8,128)(2,1)} %param.14) | copy-start | bytes 294916
  75.8 8.7 %copy-start.6 = (bf16[4,128]{1,0:T(4,128)(2,1)S(1)}, bf16[4,128]{1,0:T(4,128)(2,1)}, u32[]{:S(2)}) copy-start(bf16[4,128]{1,0:T(4,128)(2,1)} %param.15) | copy-start | bytes 3076
  77.0 21.9 %all-to-all-start.2 = ((bf16[16,272,128]{2,1,0:T(8,128)(2,1)}), bf16[16,272,128]{2,1,0:T(8,128)(2,1)S(1)}, u32[]{:S(2)}, u32[]{:S(2)}) async-start(bf16[16,272,128]{2,1,0:T(8,128)(2,1)} %broadcast_in_dim.32), calls=%async_computation.2 | async-start | bytes 2228224 | tf_op jit(solution)/shard_map/all_to_all | solution.py:219
  98.9 1.1 copy-start.1
  137.5 10.9 %all-to-all-start.3 = ((bf16[4,128,512]{2,1,0:T(8,128)(2,1)}), bf16[4,128,512]{2,1,0:T(8,128)(2,1)S(1)}, u32[]{:S(2)}, u32[]{:S(2)}) async-start(bf16[4,128,512]{2,1,0:T(8,128)(2,1)} %bitcast.44), calls=%async_computation.3 | async-start | bytes 1048576 | tf_op jit(solution)/shard_map/all_to_all | solution.py:219
  152.2 20.9 %all-to-all-start.4 = ((bf16[16,128,128]{2,1,0:T(8,128)(2,1)}), bf16[16,128,128]{2,1,0:T(8,128)(2,1)S(1)}, u32[]{:S(2)}, u32[]{:S(2)}) async-start(bf16[16,128,128]{2,1,0:T(8,128)(2,1)} %bitcast.12), calls=%async_computation.4 | async-start | bytes 1048576 | tf_op jit(solution)/shard_map/all_to_all | solution.py:219
  173.1 1.9 copy-start.2
  175.0 35.0 %all-to-all-start.5 = ((bf16[64,128,128]{2,1,0:T(8,128)(2,1)}), bf16[64,128,128]{2,1,0:T(8,128)(2,1)S(1)}, u32[]{:S(2)}, u32[]{:S(2)}) async-start(bf16[64,128,128]{2,1,0:T(8,128)(2,1)} %bitcast.41), calls=%async_computation.5 | async-start | bytes 4194304 | tf_op jit(solution)/shard_map/all_to_all | solution.py:219
  210.0 1.4 copy-start

commit v3 on v2

--- a/solution.py
+++ b/solution.py
@@ -9,7 +9,6 @@
 XY = ("x", "y")
 FEAT = ("zl", "core")
 KEY_GROUP = ("x", "y", "zl", "core")
-QUERY_GROUP = ("zh", "zl", "core")
 FOLD_PENALTY = 16384.0
 
 epsilon = 1e-06
@@ -31,39 +30,62 @@
     return lax.dot_general(a, b, (((1,), (1,)), ((), ())), preferred_element_type=jnp.float32)
 
 
-def induce_kernel(x_ref, bias_ref, proj_ref, points_ref, cells_ref, sums_ref, stage_ref):
+def induce_kernel(
+    x_ref, bias_ref, proj_ref, points_ref, order_ref, cells_ref, sums_ref, kv_ref, values_ref, weights_ref
+):
     chunk, feats, embed = x_ref.shape
     step = pl.program_id(0)
-    stage_ref[...] = x_ref[...].astype(jnp.float32).reshape(chunk * feats, embed)
     first = pl.multiple_of(step * chunk, chunk)
-    for f in range(feats):
-        cells_ref[f, pl.ds(first, chunk), :] = stage_ref[
-            pl.ds(f, chunk, stride=feats), :
-        ].astype(jnp.bfloat16)
+    order = order_ref[...]
+    for r in range(0, chunk, 16):
+        low = x_ref[r : r + 8].reshape(8 * feats, embed)
+        high = x_ref[r + 8 : r + 16].reshape(8 * feats, embed)
+        moved = product(order, jnp.concatenate([low, high], axis=1))
+        low = moved[:, :embed].reshape(feats, 8, embed)
+        high = moved[:, embed:].reshape(feats, 8, embed)
+        cells_ref[:, pl.ds(first + r, 16), :] = jnp.concatenate([low, high], axis=1).astype(
+            jnp.bfloat16
+        )
 
     @pl.when(step == pl.num_programs(0) - 1)
     def _():
         points = points_ref[...]
-        ones = jnp.ones((8, embed), jnp.bfloat16)
         bias = bias_ref[0:1, :]
-
-        def feature(f, carry):
-            kv = product(cells_ref[f], proj_ref[...]).astype(jnp.bfloat16)
-            keys = kv[:, :embed]
-            wide = keys.astype(jnp.float32)
-            squares = product_nt(ones, (wide * wide).astype(jnp.bfloat16))
-            factor = lax.rsqrt(squares * (1.0 / embed) + epsilon) * (score_scale * LOG2E)
-            scores = product_nt(points, keys) * factor[0:1, :] + bias
-            weights = jnp.exp2(scores).astype(jnp.bfloat16)
-            sums_ref[f] = product(weights, kv[:, embed:]).astype(jnp.bfloat16)
+        pair = 4
+
+        def project(f, slot):
+            kv_ref[slot] = product(cells_ref[f], proj_ref[...]).astype(jnp.bfloat16)
+
+        def weigh(slot):
+            keys = kv_ref[slot, :, :embed].astype(jnp.float32)
+            factor = lax.rsqrt(jnp.mean(keys * keys, axis=-1, keepdims=True) + epsilon)
+            keys = (keys * (factor * (score_scale * LOG2E))).astype(jnp.bfloat16)
+            values_ref[slot] = kv_ref[slot, :, embed:]
+            weights_ref[slot] = jnp.exp2(product_nt(points, keys) + bias).astype(jnp.bfloat16)
+
+        def add_up(f, slot):
+            sums_ref[f] = product(weights_ref[slot], values_ref[slot]).astype(jnp.bfloat16)
+
+        def features(i, carry):
+            for j in range(pair):
+                ahead = jnp.minimum(i * pair + j + 1, feats - 1)
+                add_up(jnp.maximum(i * pair + j - 1, 0), 1 - j % 2)
+                project(ahead, 1 - j % 2)
+                weigh(j % 2)
             return carry
 
-        lax.fori_loop(0, feats, feature, 0, unroll=4)
+        project(0, 0)
+        lax.fori_loop(0, feats // pair, features, 0)
+        add_up(feats - 1, 1)
 
 
 def induce(table_cells, bias, induce_proj, induce_norm, chunk=64):
     rows, feats, embed = table_cells.shape
     points = induce_norm.shape[0]
+    place = jnp.arange(8 * feats)
+    order = ((place[:, None] % 8) * feats + place[:, None] // 8 == place[None, :]).astype(
+        jnp.bfloat16
+    )
     return pl.pallas_call(
         induce_kernel,
         out_shape=(
@@ -76,14 +98,19 @@
             pl.BlockSpec(bias.shape, lambda i: (0, 0)),
             pl.BlockSpec(induce_proj.shape, lambda i: (0, 0)),
             pl.BlockSpec(induce_norm.shape, lambda i: (0, 0)),
+            pl.BlockSpec(order.shape, lambda i: (0, 0)),
         ],
         out_specs=(
             pl.BlockSpec((feats, rows, embed), lambda i: (0, 0, 0)),
             pl.BlockSpec((feats, points, embed), lambda i: (0, 0, 0)),
         ),
-        scratch_shapes=[pltpu.VMEM((chunk * feats, embed), jnp.float32)],
+        scratch_shapes=[
+            pltpu.VMEM((2, rows, 2 * embed), jnp.bfloat16),
+            pltpu.VMEM((2, rows, embed), jnp.bfloat16),
+            pltpu.VMEM((2, points, rows), jnp.bfloat16),
+        ],
         name="induce",
-    )(table_cells, bias, induce_proj, induce_norm)
+    )(table_cells, bias, induce_proj, induce_norm, order)
 
 
 def cell_query_kernel(x_ref, proj_ref, o_ref):
@@ -108,48 +135,80 @@
 
 
 def summary_kernel(
-    induced_ref, cells_ref, query_ref, back_ref, row_ref, summary_ref, permute_ref, o_ref, total_ref
+    induced_ref,
+    cells_ref,
+    query_ref,
+    back_ref,
+    row_ref,
+    summary_ref,
+    spread_ref,
+    permute_ref,
+    o_ref,
+    expos_ref,
+    point_ref,
+    updated_ref,
+    values_ref,
+    weights_ref,
+    total_ref,
 ):
     step = pl.program_id(0)
     feats, rows, embed = cells_ref.shape
     points = embed
     summaries = total_ref.shape[1] // embed
-    back = back_ref[...]
-    row_proj = row_ref[...]
-    summary = summary_ref[...]
     ones = jnp.ones((points, embed), jnp.bfloat16)
-    parts = []
+
+    @pl.when(step == 0)
+    def _():
+        expos_ref[...] = jnp.ones_like(expos_ref)
+        point_ref[...] = jnp.zeros_like(point_ref)
+        updated_ref[...] = jnp.zeros_like(updated_ref)
+        values_ref[...] = jnp.zeros_like(values_ref)
+        weights_ref[...] = jnp.zeros_like(weights_ref)
+
+    @pl.when(step <= 3)
+    def _():
+        total_ref[...] = jnp.zeros_like(total_ref)
+
+    values = [values_ref[f].astype(jnp.float32) for f in range(feats)]
+    weights = weights_ref[...].astype(jnp.float32)
+    for c in range(summaries):
+        span = slice(c * embed, (c + 1) * embed)
+        if c < 2:
+            total_ref[:, span] += (
+                weights[:, c : c + 1] * values[0]
+                + weights[:, summaries + c : summaries + c + 1] * values[1]
+            )
+        else:
+            wide = product(weights_ref[...], spread_ref[:, 2 * c * embed : 2 * (c + 1) * embed])
+            total_ref[:, span] += wide[:, :embed] * values[0] + wide[:, embed:] * values[1]
+    row_kv = [product(updated_ref[f], row_ref[...]).astype(jnp.bfloat16) for f in range(feats)]
     for f in range(feats):
-        induced = induced_ref[0, f * points : (f + 1) * points, :]
-        point_kv = product(induced, back).astype(jnp.bfloat16)
-        point_keys = (rms_normalize(point_kv[:, :embed]) * (score_scale * LOG2E)).astype(
-            jnp.bfloat16
-        )
-        expos = jnp.exp2(product_nt(query_ref[f], point_keys)).astype(jnp.bfloat16)
-        mixed = product(expos, jnp.concatenate([point_kv[:, embed:], ones], axis=1))
+        values_ref[f] = row_kv[f][:, embed:]
+    keys = jnp.concatenate([row_kv[0][:, :embed], row_kv[1][:, :embed]], axis=1)
+    wide = keys.astype(jnp.float32)
+    squares = product((wide * wide).astype(jnp.bfloat16), summary_ref[:, embed:])
+    factor = lax.rsqrt(squares * (1.0 / embed) + epsilon) * (score_scale * LOG2E)
+    scores = product(keys, summary_ref[:, :embed]) * factor
+    weights_ref[...] = jnp.exp2(scores).astype(jnp.bfloat16)
+    for f in range(feats):
+        mixed = product(expos_ref[f], jnp.concatenate([point_ref[f], ones], axis=1))
         attended = mixed[:, :embed] / mixed[:, embed:]
-        updated = (cells_ref[f].astype(jnp.float32) + attended).astype(jnp.bfloat16)
-        row_kv = product(updated, row_proj).astype(jnp.bfloat16)
-        keys = row_kv[:, :embed]
-        wide = keys.astype(jnp.float32)
-        factor = lax.rsqrt(jnp.mean(wide * wide, axis=-1, keepdims=True) + epsilon)
-        weights = jnp.exp2(product(keys, summary) * (factor * (score_scale * LOG2E)))
-        parts.append(
-            (weights.astype(jnp.bfloat16).astype(jnp.float32), row_kv[:, embed:].astype(jnp.float32))
-        )
-    for c in range(summaries):
-        addend = parts[0][0][:, c : c + 1] * parts[0][1]
-        for weights, values in parts[1:]:
-            addend = addend + weights[:, c : c + 1] * values
-        span = slice(c * embed, (c + 1) * embed)
-
-        @pl.when(step == 0)
-        def _():
-            total_ref[:, span] = addend
-
-        @pl.when(step > 0)
-        def _():
-            total_ref[:, span] += addend
+        updated_ref[f] = (cells_ref[f].astype(jnp.float32) + attended).astype(jnp.bfloat16)
+    point_kv = product(induced_ref[0, : feats * points, :], back_ref[...]).astype(jnp.bfloat16)
+    point_keys = (rms_normalize(point_kv[:, :embed]) * (score_scale * LOG2E)).astype(jnp.bfloat16)
+    none = jnp.zeros((points, embed), jnp.bfloat16)
+    point_keys = jnp.concatenate(
+        [
+            jnp.concatenate([point_keys[:points], none], axis=1),
+            jnp.concatenate([none, point_keys[points:]], axis=1),
+        ],
+        axis=0,
+    )
+    queries = jnp.concatenate([query_ref[f] for f in range(feats)], axis=1)
+    expos = jnp.exp2(product_nt(queries, point_keys)).astype(jnp.bfloat16)
+    for f in range(feats):
+        point_ref[f] = point_kv[f * points : (f + 1) * points, embed:]
+        expos_ref[f] = expos[:, f * points : (f + 1) * points]
 
     @pl.when(step == pl.num_programs(0) - 1)
     def _():
@@ -158,26 +217,46 @@
         )
 
 
-def summarize(induced, cells, queries, back, row_proj, summary, permute, summaries, step=2):
+def summarize(induced, cells, queries, back, row_proj, summary, permute, summaries, pair=2):
     feats, rows, embed = cells.shape
     width = summaries * embed
+    steps = feats // pair
+    lane = jnp.arange(embed)
+    owner = lane // summaries
+    scored = [jnp.where(owner[None] == f, jnp.tile(summary, (1, embed // summaries)), 0) for f in range(pair)]
+    squared = [jnp.broadcast_to(owner[None] == f, (embed, embed)) for f in range(pair)]
+    both = jnp.concatenate(
+        [jnp.concatenate(scored, axis=0), jnp.concatenate(squared, axis=0).astype(jnp.bfloat16)],
+        axis=1,
+    )
+    source = jnp.arange(summaries * pair)
+    source = (source % pair) * summaries + source // pair
+    spread = (lane[:, None] == jnp.repeat(source, embed)[None]).astype(jnp.bfloat16)
     return pl.pallas_call(
         summary_kernel,
         out_shape=jax.ShapeDtypeStruct((rows, width), jnp.bfloat16),
-        grid=(feats // step,),
+        grid=(steps + 3,),
         in_specs=[
-            pl.BlockSpec((1,) + induced.shape[1:], lambda i: (i, 0, 0)),
-            pl.BlockSpec((step, rows, embed), lambda i: (i, 0, 0)),
-            pl.BlockSpec((step, rows, embed), lambda i: (i, 0, 0)),
+            pl.BlockSpec((1,) + induced.shape[1:], lambda i: (jnp.minimum(i, steps - 1), 0, 0)),
+            pl.BlockSpec((pair, rows, embed), lambda i: (jnp.clip(i - 1, 0, steps - 1), 0, 0)),
+            pl.BlockSpec((pair, rows, embed), lambda i: (jnp.minimum(i, steps - 1), 0, 0)),
             pl.BlockSpec(back.shape, lambda i: (0, 0)),
             pl.BlockSpec(row_proj.shape, lambda i: (0, 0)),
-            pl.BlockSpec(summary.shape, lambda i: (0, 0)),
+            pl.BlockSpec(both.shape, lambda i: (0, 0)),
+            pl.BlockSpec(spread.shape, lambda i: (0, 0)),
             pl.BlockSpec(permute.shape, lambda i: (0, 0)),
         ],
         out_specs=pl.BlockSpec((rows, width), lambda i: (0, 0)),
-        scratch_shapes=[pltpu.VMEM((rows, width), jnp.float32)],
+        scratch_shapes=[
+            pltpu.VMEM((pair, rows, embed), jnp.bfloat16),
+            pltpu.VMEM((pair, embed, embed), jnp.bfloat16),
+            pltpu.VMEM((pair, rows, embed), jnp.bfloat16),
+            pltpu.VMEM((pair, rows, embed), jnp.bfloat16),
+            pltpu.VMEM((rows, embed), jnp.bfloat16),
+            pltpu.VMEM((rows, width), jnp.float32),
+        ],
         name="summarize",
-    )(induced, cells, queries, back, row_proj, summary, permute)
+    )(induced, cells, queries, back, row_proj, both, spread, permute)
 
 
 def attention_kernel(q_ref, qm_ref, kv_ref, km_ref, o_ref, *, groups):
@@ -199,7 +278,7 @@
     o_ref[...] = total.astype(o_ref.dtype)
 
 
-def attention(q, q_marks, kv, k_marks, query_block=512, groups=8):
+def attention(q, q_marks, kv, k_marks, query_block=1024, groups=8):
     queries, dim = q.shape
     return pl.pallas_call(
         lambda *refs: attention_kernel(*refs, groups=groups),
@@ -246,8 +325,15 @@
     block = rows_here // feat_devices
     half = block // 2
 
-    proj_pair = jnp.concatenate([context_proj, other(context_proj, "core")], axis=2)
-    proj_full = jnp.concatenate([proj_pair, other(proj_pair, "zl")], axis=2)
+    proj_full = jnp.concatenate(
+        [
+            context_proj,
+            other(context_proj, "core"),
+            other(context_proj, "zl"),
+            lax.ppermute(context_proj, FEAT, [(i, 3 - i) for i in range(4)]),
+        ],
+        axis=2,
+    )
 
     labelled = (train_mask == 1).astype(jnp.bfloat16)
     index = jnp.arange(rows_here)
@@ -270,8 +356,8 @@
     cells, numerator = induce(table_cells, bias, induce_proj, induce_norm)
     points = inducing.shape[0]
     share_xy = feats_here * points // groups_xy
+    numerator, proj_full = lax.optimization_barrier((numerator, proj_full))
     part = exchange(numerator.reshape(groups_xy, share_xy, embed), XY)
-    part, proj_full = lax.optimization_barrier((part, proj_full))
     part = jnp.sum(part.astype(jnp.float32), axis=0).astype(jnp.bfloat16)
     queries = cell_queries(cells, induce_back[:, :embed])
     sent = jnp.concatenate([part, jnp.pad(codes, ((0, 12), (0, 0)))], axis=0)
@@ -285,7 +371,6 @@
 
     summary = rms_normalize(summary_query).astype(jnp.bfloat16).T
     summaries = summary.shape[1]
-    summary = jnp.pad(summary, ((0, 0), (0, embed - summaries)))
     ordered = summarize(
         got, cells, queries, induce_back[:, embed:], row_proj, summary, permute, summaries
     )
@@ -299,24 +384,33 @@
         preferred_element_type=jnp.float32,
     ).astype(jnp.bfloat16)
 
+    def placed(value):
+        value = jnp.where(zl == 0, value, value[::-1])
+        return jnp.where(core == 0, value, value[:, ::-1])
+
     def heads(value):
         value = value.reshape(-1, 2, 2, HEAD_DIM).transpose(1, 2, 0, 3)
-        value = jnp.where(zl == 0, value, value[::-1])
-        return jnp.where(core == 0, value, value[:, ::-1]).reshape(
-            feat_devices, -1, HEAD_DIM
-        )
-
-    q = (rms_normalize(heads(projected[0])) * (score_scale * LOG2E)).astype(jnp.bfloat16)
+        return placed(value).reshape(feat_devices, -1, HEAD_DIM)
+
     k = rms_normalize(heads(projected[1][:half])).astype(jnp.bfloat16)
     v = heads(projected[2][:half])
-    q_all = exchange(
-        jnp.broadcast_to(q[None], (groups_z,) + q.shape).reshape(-1, block, HEAD_DIM), QUERY_GROUP
-    ).reshape(-1, HEAD_DIM)
     kv = jnp.concatenate([k, v], axis=1)
     kv_all = exchange(
         jnp.broadcast_to(kv[None], (groups_xy,) + kv.shape).reshape(-1, 2 * half, HEAD_DIM),
         KEY_GROUP,
     )
+    q = rms_normalize(projected[0].reshape(block, feat_devices, HEAD_DIM))
+    q = (q * (score_scale * LOG2E)).astype(jnp.bfloat16).transpose(1, 0, 2)
+    q = q.reshape(2, 2, block, HEAD_DIM)
+    q = jnp.stack([q[:, 0], other(q[:, 1], "core")], axis=1)
+    q = placed(jnp.stack([q[0], other(q[1], "zl")], axis=0)).reshape(rows_here, HEAD_DIM)
+    shifted = [q] + [
+        lax.ppermute(q, "zh", [(i, (i + k) % groups_z) for i in range(groups_z)])
+        for k in range(1, groups_z)
+    ]
+    shifted = jnp.stack(shifted[::-1] + shifted[:0:-1])
+    q_all = lax.dynamic_slice_in_dim(shifted, groups_z - 1 - zh, groups_z, 0)
+    q_all = q_all.reshape(-1, HEAD_DIM)
     query_codes = lax.dynamic_index_in_dim(all_codes, xy, 0, keepdims=False).reshape(-1)
     key_codes = lax.dynamic_index_in_dim(all_codes, zh, 1, keepdims=False)[..., :half].reshape(-1)
     lanes = jnp.arange(HEAD_DIM).astype(jnp.float32)

time: 249 us -> 222 us (0.89); the launches traced: 244 us -> 220 us
  Pallas kernels: 85.2 us -> 65.4 us
  blocking collectives: 36.1 us -> 19 us
  starting transfers between devices: 30.8 us -> 38.5 us
  waiting for transfers between devices: 67.6 us -> 71.3 us
  other arithmetic: 9.69 us -> 12.2 us
    all_to_all x2 -> x1, blocking collectives: 36.1 us -> 19 us  [exchange(): return lax.all_to_all(value, axes, 0, 0, tiled=True)]
    ppermute x0 -> x4, waiting for transfers between devices: none -> 13.5 us  [the longest x3 13.5 us: local(): lax.ppermute(q, 'zh', [(i, (i + k) % groups_z) for i in range(groups_z)])]
    all_to_all x5, waiting for transfers between devices: 48.5 us -> 35.3 us  [exchange(): return lax.all_to_all(value, axes, 0, 0, tiled=True)]
    pallas_call x1, Pallas kernels: 37.4 us -> 26.4 us  [summarize(): pl.pallas_call(summary_kernel, out_shape=jax.ShapeDtypeStruct((rows, widt...]
    pallas_call x1, Pallas kernels: 25.7 us -> 17.5 us  [induce(): pl.pallas_call(induce_kernel, out_shape=(jax.ShapeDtypeStruct((feats, row...]
    ppermute x0 -> x4, starting transfers between devices: none -> 5.77 us  [the longest x3 5.77 us: local(): lax.ppermute(q, 'zh', [(i, (i + k) % groups_z) for i in range(groups_z)])]
    ppermute x2 -> x4, waiting for transfers between devices: 19.1 us -> 22.4 us  [other(): return lax.ppermute(value, axis, [(0, 1), (1, 0)])]
    ppermute x2 -> x4, starting transfers between devices: 0.18 us -> 2.8 us  [other(): return lax.ppermute(value, axis, [(0, 1), (1, 0)])]
  transfers between devices with their start and end apart: 7 -> 13, of which waited for: 5 -> 7; matrix products, arithmetic and copies ran while one was open for 5% -> 7% of each run, Pallas kernels for 14% -> 12%
where the time goes in v3:
time: 222 us; the launch traced here: 220 us
  waiting for transfers between devices  71.3 us (32%)
  Pallas kernels  65.4 us (29%)
  starting transfers between devices  38.5 us (17%)
  blocking collectives  19 us (9%)
  other arithmetic  12.2 us (5%)
  local copies, waits for them, and re-layouts  11.6 us (5%)
    all_to_all x5, waiting for transfers between devices, exchange(): return lax.all_to_all(value, axes, 0, 0, tiled=True)  35.3 us
    all_to_all x5, starting transfers between devices, exchange(): return lax.all_to_all(value, axes, 0, 0, tiled=True)  29.9 us
    pallas_call x1, Pallas kernels, summarize(): pl.pallas_call(summary_kernel, out_shape=jax.ShapeDtypeStruct((rows, widt...  26.4 us
    ppermute x4, waiting for transfers between devices, other(): return lax.ppermute(value, axis, [(0, 1), (1, 0)])  22.4 us
    all_to_all x1, blocking collectives, exchange(): return lax.all_to_all(value, axes, 0, 0, tiled=True)  19 us
    pallas_call x1, Pallas kernels, induce(): pl.pallas_call(induce_kernel, out_shape=(jax.ShapeDtypeStruct((feats, row...  17.5 us
    ppermute x3, waiting for transfers between devices, local(): lax.ppermute(q, 'zh', [(i, (i + k) % groups_z) for i in range(groups_z)])  13.5 us
    pallas_call x1, Pallas kernels, attention(): pl.pallas_call(lambda *refs: attention_kernel(*refs, groups=groups), out_...  13.2 us
  transfers between devices with their start and end apart: 13, of which 7 were waited for; matrix products, arithmetic and copies ran while one was open for 7% of the time, Pallas kernels for 12%

profile of v3, /device:TPU:32, one launch (start us, length us, event | category | flops | bytes accessed | tf_op | source)
XLA Modules:
  0.0 220.4 jit_solution(2647358495472529105)
XLA Ops:
  0.0 1.8 collective-permute-start.1
  1.8 0.1 collective-permute-start
  1.9 0.7 broadcast_select_fusion.6
  2.6 0.9 fusion.16
  3.5 0.8 fusion.10.order_ref
  4.3 0.7 convert_element_type.135
  5.0 1.4 fusion.17.points_ref
  6.4 0.6 broadcast_in_dim.52.bias_ref
  7.0 17.5 %induce.1 = (bf16[32,512,128]{2,1,0:T(8,128)(2,1)}, bf16[32,128,128]{2,1,0:T(8,128)(2,1)}) custom-call(bf16[512,32,128]{2,1,0:T(8,128)(2,1)} %x_ref.1, f32[8,512]{1,0:T(8,128)} %broadcast_in_dim.52.bias_ref, bf16[128,256]{1,0:T(8,128)(2,1)} %proj_ref.1, bf16[128,128]{1,0:T(8,128)(2,1)} %fusion.17.points_ref, bf16[256,256]{1,0:T(8,128)(2,1)} %fusion.10.order_ref), custom_call_target="tpu_custom_call" | custom-call | tf_op jit(solution)/shard_map/induce/pallas_call | solution.py:89
  24.6 0.2 pad_maximum_fusion
  24.8 7.0 %all-to-all-start = ((bf16[16,256,128]{2,1,0:T(8,128)(2,1)}), bf16[16,256,128]{2,1,0:T(8,128)(2,1)S(1)}, u32[]{:S(2)}, u32[]{:S(2)}) async-start(bf16[16,256,128]{2,1,0:T(8,128)(2,1)} %bitcast.66), calls=%async_computation | async-start | bytes 2097152 | tf_op jit(solution)/shard_map/all_to_all | solution.py:298
  31.8 0.1 fusion.21
  31.9 0.2 fusion.3
  32.1 0.3 fusion.2
  32.4 17.5 %all-to-all-done = bf16[16,256,128]{2,1,0:T(8,128)(2,1)S(1)} async-done(((bf16[16,256,128]{2,1,0:T(8,128)(2,1)}), bf16[16,256,128]{2,1,0:T(8,128)(2,1)S(1)}, u32[]{:S(2)}, u32[]{:S(2)}) %all-to-all-start) | async-done | bytes 1048608 | tf_op jit(solution)/shard_map/all_to_all | solution.py:298
  49.9 0.1 reduce_sum.103
  50.0 0.7 broadcast_in_dim.53
  50.8 7.6 %all-to-all-start.1 = ((bf16[4,272,128]{2,1,0:T(8,128)(2,1)}), bf16[4,272,128]{2,1,0:T(8,128)(2,1)S(1)}, u32[]{:S(2)}, u32[]{:S(2)}) async-start(bf16[4,272,128]{2,1,0:T(8,128)(2,1)} %broadcast_in_dim.53), calls=%async_computation.1 | async-start | bytes 557056 | tf_op jit(solution)/shard_map/all_to_all | solution.py:298
  58.4 9.4 %all-to-all-done.1 = bf16[4,272,128]{2,1,0:T(8,128)(2,1)S(1)} async-done(((bf16[4,272,128]{2,1,0:T(8,128)(2,1)}), bf16[4,272,128]{2,1,0:T(8,128)(2,1)S(1)}, u32[]{:S(2)}, u32[]{:S(2)}) %all-to-all-start.1) | async-done | bytes 278560 | tf_op jit(solution)/shard_map/all_to_all | solution.py:298
  67.8 0.1 multiply_reduce_fusion.3
  68.0 0.1 multiply_convert_fusion.3
  68.1 1.2 broadcast_in_dim.54
  69.3 4.3 %all-to-all-start.2 = ((bf16[16,272,128]{2,1,0:T(8,128)(2,1)}), bf16[16,272,128]{2,1,0:T(8,128)(2,1)S(1)}, u32[]{:S(2)}, u32[]{:S(2)}) async-start(bf16[16,272,128]{2,1,0:T(8,128)(2,1)} %broadcast_in_dim.54), calls=%async_computation.2 | async-start | bytes 2228224 | tf_op jit(solution)/shard_map/all_to_all | solution.py:298
  73.7 0.6 slice.47.proj_ref
  74.3 0.6 slice.48.back_ref
  74.9 0.1 copy.69
  75.0 8.3 %cell_queries.1.query_ref = bf16[32,512,128]{2,1,0:T(8,128)(2,1)} custom-call(bf16[32,512,128]{2,1,0:T(8,128)(2,1)} %get-tuple-element.12.x_ref.cells_ref, bf16[128,128]{1,0:T(8,128)(2,1)} %slice.47.proj_ref), custom_call_target="tpu_custom_call" | custom-call | tf_op jit(solution)/shard_map/cell_queries/pallas_call | solution.py:124
  83.4 0.7 pad_maximum_fusion.1.summary_ref
  84.1 0.8 fusion.6.spread_ref
  84.9 0.9 fusion.1.permute_ref
  85.8 2.2 all-to-all-done.2.induced_ref
  88.0 1.1 copy-done.1
  89.1 26.4 %summarize.1 = bf16[512,512]{1,0:T(8,128)(2,1)} custom-call(bf16[16,272,128]{2,1,0:T(8,128)(2,1)} %copy-done.1, bf16[32,512,128]{2,1,0:T(8,128)(2,1)} %get-tuple-element.12.x_ref.cells_ref, bf16[32,512,128]{2,1,0:T(8,128)(2,1)} %cell_queries.1.query_ref, bf16[128,256]{1,0:T(8,128)(2,1)} %slice.48.back_ref, bf16[128,256]{1,0:T(8,128)(2,1)} %row_ref.1, ...), custom_call_target="tpu_custom_call" | custom-call | tf_op jit(solution)/shard_map/summarize/pallas_call | solution.py:235
  115.5 4.6 %all-to-all-start.3 = ((bf16[4,128,512]{2,1,0:T(8,128)(2,1)}), bf16[4,128,512]{2,1,0:T(8,128)(2,1)S(1)}, u32[]{:S(2)}, u32[]{:S(2)}) async-start(bf16[4,128,512]{2,1,0:T(8,128)(2,1)} %bitcast.64), calls=%async_computation.3 | async-start | bytes 1048576 | tf_op jit(solution)/shard_map/all_to_all | solution.py:298
  120.1 0.8 slice.65
  121.1 6.2 %all-to-all-done.3 = bf16[4,128,512]{2,1,0:T(8,128)(2,1)S(1)} async-done(((bf16[4,128,512]{2,1,0:T(8,128)(2,1)}), bf16[4,128,512]{2,1,0:T(8,128)(2,1)S(1)}, u32[]{:S(2)}, u32[]{:S(2)}) %all-to-all-start.3) | async-done | bytes 524320 | tf_op jit(solution)/shard_map/all_to_all | solution.py:298
  127.5 0.2 reduce_sum.108
  127.7 0.2 mul.133
  127.9 0.4 fusion
  128.5 0.2 multiply_reduce_fusion.1
  128.9 0.3 rev.23
  129.3 0.3 rev.21
  129.6 0.1 broadcast_select_fusion.2
  129.7 0.3 multiply_reduce_fusion.2
  130.1 0.1 copy.76
  130.2 0.1 multiply_convert_fusion.2
  130.5 1.9 broadcast_in_dim.61
  132.3 6.5 %all-to-all-start.4 = ((bf16[64,128,128]{2,1,0:T(8,128)(2,1)}), bf16[64,128,128]{2,1,0:T(8,128)(2,1)S(1)}, u32[]{:S(2)}, u32[]{:S(2)}) async-start(bf16[64,128,128]{2,1,0:T(8,128)(2,1)} %bitcast.61), calls=%async_computation.4 | async-start | bytes 4194304 | tf_op jit(solution)/shard_map/all_to_all | solution.py:298
  138.8 0.1 fusion.9
  139.0 0.4 collective-permute-start.3
  139.4 1.6 compare_convert_fusion.refs_3_
  141.0 0.5 collective-permute-start.4
  141.5 22.4 %collective-permute-done.4 = bf16[2,128,128]{2,1,0:T(8,128)(2,1)S(1)} collective-permute-done((bf16[2,128,128]{2,1,0:T(8,128)(2,1)S(1)}, bf16[2,128,128]{2,1,0:T(8,128)(2,1)S(1)}, u32[]{:S(2)}, u32[]{:S(2)}) %collective-permute-start.4) | collective-permute-done | bytes 65568 | tf_op jit(solution)/shard_map/ppermute | solution.py:302
  164.0 2.4 %collective-permute-start.5 = (bf16[512,128]{1,0:T(8,128)(2,1)S(1)}, bf16[512,128]{1,0:T(8,128)(2,1)S(1)}, u32[]{:S(2)}, u32[]{:S(2)}) collective-permute-start(bf16[512,128]{1,0:T(8,128)(2,1)S(1)} %bitcast.73), channel_id=1, source_target_pairs={{0,48},{16,0},{32,16},{48,32},{1,49},{17,1},{33,17},{49,33},{2,50}... | collective-permute-start | bytes 393224 | tf_op jit(solution)/shard_map/ppermute | solution.py:408
  166.4 1.1 select_convert_fusion.refs_1_
  167.5 3.4 %collective-permute-start.6 = (bf16[512,128]{1,0:T(8,128)(2,1)S(1)}, bf16[512,128]{1,0:T(8,128)(2,1)S(1)}, u32[]{:S(2)}, u32[]{:S(2)}) collective-permute-start(bf16[512,128]{1,0:T(8,128)(2,1)S(1)} %bitcast.74), channel_id=1, source_target_pairs={{0,32},{16,48},{32,0},{48,16},{1,33},{17,49},{33,1},{49,17},{2,34}... | collective-permute-start | bytes 393224 | tf_op jit(solution)/shard_map/ppermute | solution.py:408
  170.9 10.2 %collective-permute-done.6 = bf16[512,128]{1,0:T(8,128)(2,1)S(1)} collective-permute-done((bf16[512,128]{1,0:T(8,128)(2,1)S(1)}, bf16[512,128]{1,0:T(8,128)(2,1)S(1)}, u32[]{:S(2)}, u32[]{:S(2)}) %collective-permute-start.6) | collective-permute-done | bytes 131104 | tf_op jit(solution)/shard_map/ppermute | solution.py:408
  181.1 3.4 %collective-permute-done.7 = bf16[512,128]{1,0:T(8,128)(2,1)S(1)} collective-permute-done((bf16[512,128]{1,0:T(8,128)(2,1)S(1)}, bf16[512,128]{1,0:T(8,128)(2,1)S(1)}, u32[]{:S(2)}, u32[]{:S(2)}) %collective-permute-start.7) | collective-permute-done | bytes 131104 | tf_op jit(solution)/shard_map/ppermute | solution.py:408
  184.6 0.8 constant_dynamic-slice_fusion.1
  185.4 1.4 copy-done
  186.8 13.2 %attention.1 = bf16[2048,128]{1,0:T(8,128)(2,1)} custom-call(bf16[2048,128]{1,0:T(8,128)(2,1)} %bitcast.63, bf16[2048,128]{1,0:T(8,128)(2,1)} %select_convert_fusion.refs_1_, bf16[64,128,128]{2,1,0:T(8,128)(2,1)} %copy-done, bf16[4096,128]{1,0:T(8,128)(2,1)} %compare_convert_fusion.refs_3_), custom_call_target="tpu_custom_call" | custom-call | tf_op jit(solution)/shard_map/attention/pallas_call | solution.py:283
  200.0 19.0 %all_to_all.30 = bf16[4,512,128]{2,1,0:T(8,128)(2,1)S(1)} all-to-all(bf16[4,512,128]{2,1,0:T(8,128)(2,1)} %bitcast.62), channel_id=1, replica_groups=mesh['x'=4,'zh'=4,'y'=4,'zl'=2,'core'=2] {'zh'}, dimensions={0} | all-to-all | bytes 1048576 | tf_op jit(solution)/shard_map/all_to_all | solution.py:298
  219.0 0.1 multiply_reduce_fusion
  219.2 1.2 convolution_convert_fusion.1
  (74 shorter events, 1.6 us)
Async XLA Ops:
  0.0 24.6 %collective-permute-start.2 = (bf16[3,512,128]{2,1,0:T(8,128)(2,1)}, bf16[3,512,128]{2,1,0:T(8,128)(2,1)S(1)}, u32[]{:S(2)}, u32[]{:S(2)}) collective-permute-start(bf16[3,512,128]{2,1,0:T(8,128)(2,1)} %param.17), channel_id=1, source_target_pairs={{0,3},{1,2},{2,1},{3,0},{4,7},{5,6},{6,5},{7,4},{8,11},{9,10},{10,... | collective-permute-start | bytes 1179656 | tf_op jit(solution)/shard_map/ppermute | solution.py:333
  0.0 24.6 %collective-permute-start.1 = (bf16[3,512,128]{2,1,0:T(8,128)(2,1)}, bf16[3,512,128]{2,1,0:T(8,128)(2,1)S(1)}, u32[]{:S(2)}, u32[]{:S(2)}) collective-permute-start(bf16[3,512,128]{2,1,0:T(8,128)(2,1)} %param.17), channel_id=1, source_target_pairs={{0,2},{2,0},{1,3},{3,1},{4,6},{6,4},{5,7},{7,5},{8,10},{10,8},{9,1... | collective-permute-start | bytes 1179656 | tf_op jit(solution)/shard_map/ppermute | solution.py:302
  1.8 22.8 %collective-permute-start = (bf16[3,512,128]{2,1,0:T(8,128)(2,1)}, bf16[3,512,128]{2,1,0:T(8,128)(2,1)S(1)}, u32[]{:S(2)}, u32[]{:S(2)}) collective-permute-start(bf16[3,512,128]{2,1,0:T(8,128)(2,1)} %param.17), channel_id=1, source_target_pairs={{0,1},{1,0},{2,3},{3,2},{4,5},{5,4},{6,7},{7,6},{8,9},{9,8},{10,11... | collective-permute-start | bytes 1179656 | tf_op jit(solution)/shard_map/ppermute | solution.py:302
  7.0 17.6 %copy-start.2 = (bf16[3,512,128]{2,1,0:T(8,128)(2,1)S(1)}, bf16[3,512,128]{2,1,0:T(8,128)(2,1)}, u32[]{:S(2)}) copy-start(bf16[3,512,128]{2,1,0:T(8,128)(2,1)} %param.17) | copy-start | bytes 1179652
  24.6 7.2 %copy-start.4 = (bf16[4,128]{1,0:T(4,128)(2,1)S(1)}, bf16[4,128]{1,0:T(4,128)(2,1)}, u32[]{:S(2)}) copy-start(bf16[4,128]{1,0:T(4,128)(2,1)} %param.15) | copy-start | bytes 3076
  24.8 25.1 %all-to-all-start = ((bf16[16,256,128]{2,1,0:T(8,128)(2,1)}), bf16[16,256,128]{2,1,0:T(8,128)(2,1)S(1)}, u32[]{:S(2)}, u32[]{:S(2)}) async-start(bf16[16,256,128]{2,1,0:T(8,128)(2,1)} %bitcast.66), calls=%async_computation | async-start | bytes 2097152 | tf_op jit(solution)/shard_map/all_to_all | solution.py:298
  50.8 17.0 %all-to-all-start.1 = ((bf16[4,272,128]{2,1,0:T(8,128)(2,1)}), bf16[4,272,128]{2,1,0:T(8,128)(2,1)S(1)}, u32[]{:S(2)}, u32[]{:S(2)}) async-start(bf16[4,272,128]{2,1,0:T(8,128)(2,1)} %broadcast_in_dim.53), calls=%async_computation.1 | async-start | bytes 557056 | tf_op jit(solution)/shard_map/all_to_all | solution.py:298
  58.4 15.2 %copy-start.3 = (bf16[128,384]{1,0:T(8,128)(2,1)S(1)}, bf16[128,384]{1,0:T(8,128)(2,1)}, u32[]{:S(2)}) copy-start(bf16[128,384]{1,0:T(8,128)(2,1)} %param.14) | copy-start | bytes 294916
  69.3 18.6 %all-to-all-start.2 = ((bf16[16,272,128]{2,1,0:T(8,128)(2,1)}), bf16[16,272,128]{2,1,0:T(8,128)(2,1)S(1)}, u32[]{:S(2)}, u32[]{:S(2)}) async-start(bf16[16,272,128]{2,1,0:T(8,128)(2,1)} %broadcast_in_dim.54), calls=%async_computation.2 | async-start | bytes 2228224 | tf_op jit(solution)/shard_map/all_to_all | solution.py:298
  88.0 1.1 copy-start.1
  115.5 11.8 %all-to-all-start.3 = ((bf16[4,128,512]{2,1,0:T(8,128)(2,1)}), bf16[4,128,512]{2,1,0:T(8,128)(2,1)S(1)}, u32[]{:S(2)}, u32[]{:S(2)}) async-start(bf16[4,128,512]{2,1,0:T(8,128)(2,1)} %bitcast.64), calls=%async_computation.3 | async-start | bytes 1048576 | tf_op jit(solution)/shard_map/all_to_all | solution.py:298
  132.3 53.1 %all-to-all-start.4 = ((bf16[64,128,128]{2,1,0:T(8,128)(2,1)}), bf16[64,128,128]{2,1,0:T(8,128)(2,1)S(1)}, u32[]{:S(2)}, u32[]{:S(2)}) async-start(bf16[64,128,128]{2,1,0:T(8,128)(2,1)} %bitcast.61), calls=%async_computation.4 | async-start | bytes 4194304 | tf_op jit(solution)/shard_map/all_to_all | solution.py:298
  139.0 2.0 collective-permute-start.3
  141.0 22.9 %collective-permute-start.4 = (bf16[2,128,128]{2,1,0:T(8,128)(2,1)S(1)}, bf16[2,128,128]{2,1,0:T(8,128)(2,1)S(1)}, u32[]{:S(2)}, u32[]{:S(2)}) collective-permute-start(bf16[2,128,128]{2,1,0:T(8,128)(2,1)S(1)} %get-tuple-element.20), channel_id=1, source_target_pairs={{0,2},{2,0},{1,3},{3,1},{4,6},{6,4},{5,7},{7,5},{8,10},{10,8},{9,1... | collective-permute-start | bytes 196616 | tf_op jit(solution)/shard_map/ppermute | solution.py:302
  164.0 6.9 %collective-permute-start.5 = (bf16[512,128]{1,0:T(8,128)(2,1)S(1)}, bf16[512,128]{1,0:T(8,128)(2,1)S(1)}, u32[]{:S(2)}, u32[]{:S(2)}) collective-permute-start(bf16[512,128]{1,0:T(8,128)(2,1)S(1)} %bitcast.73), channel_id=1, source_target_pairs={{0,48},{16,0},{32,16},{48,32},{1,49},{17,1},{33,17},{49,33},{2,50}... | collective-permute-start | bytes 393224 | tf_op jit(solution)/shard_map/ppermute | solution.py:408
  167.5 13.6 %collective-permute-start.6 = (bf16[512,128]{1,0:T(8,128)(2,1)S(1)}, bf16[512,128]{1,0:T(8,128)(2,1)S(1)}, u32[]{:S(2)}, u32[]{:S(2)}) collective-permute-start(bf16[512,128]{1,0:T(8,128)(2,1)S(1)} %bitcast.74), channel_id=1, source_target_pairs={{0,32},{16,48},{32,0},{48,16},{1,33},{17,49},{33,1},{49,17},{2,34}... | collective-permute-start | bytes 393224 | tf_op jit(solution)/shard_map/ppermute | solution.py:408
  170.9 13.6 %collective-permute-start.7 = (bf16[512,128]{1,0:T(8,128)(2,1)S(1)}, bf16[512,128]{1,0:T(8,128)(2,1)S(1)}, u32[]{:S(2)}, u32[]{:S(2)}) collective-permute-start(bf16[512,128]{1,0:T(8,128)(2,1)S(1)} %bitcast.75), channel_id=1, source_target_pairs={{0,16},{16,32},{32,48},{48,0},{1,17},{17,33},{33,49},{49,1},{2,18}... | collective-permute-start | bytes 393224 | tf_op jit(solution)/shard_map/ppermute | solution.py:408
  185.4 1.4 copy-start
